TPU v7x, 32 devices: a whole 2x2x4 slice. The times are simulated.
32 devices in a mesh: gx: 4 (over z), gy: 8 (over y, x, core).
Axes of the slice: x: 2, y: 2, z: 4, core: 2. Of those that a mesh axis runs over, the one named last changes fastest.
Arguments:
- object_field: float32 [2, 2, 512, 1024], P(None, None, 'gx', 'gy'), may hold values from -1 to 1
- probe: float32 [2, 128, 128], replicated, may hold values from -0.5 to 0.5
- propagator: float32 [128, 128], replicated, may hold values from -3.140625 to 3.140625
- offsets: int32 [4, 8, 12, 2], P('gx', 'gy'), may hold values from 0 to 128
- counts: int32 [4, 8], P('gx', 'gy'), may hold values from 1 to 12, as said below
- intensity: float32 [4, 8, 12, 128, 128], P('gx', 'gy'), may hold values from 0.1 to 4
Outputs:
- updated_object: float32 [2, 2, 512, 1024], P(None, None, 'gx', 'gy')
Inputs may be any that keep to these rules, and one draw needn't show every extreme that they name: `counts`: some tile has all 12 slots live in every draw; positions are live in slot order.
All inputs are finite; a program needn't handle non-finite values.
Results may differ from a plain program's by a relative error of at most 0.0003.
Values sent between devices are 32-bit elements; how exact they have to be, the bound alone decides.
No kernel may reach another device: no remote copies, remote signals or barrier semaphores. Data moves between devices by JAX's collectives and lax.ppermute only.
A program may use at most 64 MiB of HBM per device.

v0:
```python
import functools
import math

import jax
import jax.numpy as jnp
import numpy as np
from jax import lax
from jax.experimental import pallas as pl
from jax.experimental.pallas import tpu as pltpu
from jax.sharding import PartitionSpec as P


BATCH = 2
NB = 6
STEP = 0.08
F32 = jnp.float32
BF16 = jnp.bfloat16


def chip_order(size):
    chips = size // 2
    return [k if 2 * k < chips else chips // 2 + chips - 1 - k for k in range(chips)]


def both(pairs):
    return [p for i, j in pairs for p in ((i, j), (j, i))]


def swap_core(value):
    size = lax.axis_size("gy")
    return lax.ppermute(value, "gy", both([(i, i + 1) for i in range(0, size, 2)]))


def swap_cols(value):
    order = chip_order(lax.axis_size("gy"))
    return lax.ppermute(value, "gy", both([(2 * i + 1, 2 * j) for i, j in zip(order, order[1:])]))


def place_tiles(value):
    order = chip_order(lax.axis_size("gy"))
    return lax.ppermute(value, "gy", [(2 * i + m, 2 * j + m) for i, j in enumerate(order) for m in range(2)])


def column(value):
    size = lax.axis_size("gx")
    parts = [value]
    for k in range(1, size):
        parts.append(lax.ppermute(value, "gx", [(i, (i + k) % size) for i in range(size)]))
    return parts


def dft_tables(n):
    index = np.arange(n)
    phase = (index[:, None] * index[None, :] % n) * (2.0 * math.pi / n)
    quarters = []
    for m in (np.cos(phase) / math.sqrt(n), np.sin(phase) / math.sqrt(n)):
        m = m.astype(np.float32)
        hi = m.astype(jnp.bfloat16)
        quarters.append((jnp.asarray(hi), jnp.asarray((m - hi.astype(np.float32)).astype(jnp.bfloat16))))
    out = []
    for sign in (-1, 1):
        for c, s in zip(*quarters):
            out.append(jnp.concatenate([jnp.concatenate([c, sign * s], 1), jnp.concatenate([-sign * s, c], 1)], 0))
    return jnp.stack(out)


def split(x):
    hi = x.astype(BF16)
    return hi, (x - hi.astype(F32)).astype(BF16)


def dot(a, b):
    return jnp.dot(a, b, preferred_element_type=F32)


def right(x, tab, inverse):
    n = x[0].shape[1]
    hi, lo = split(jnp.concatenate(x, 1))
    mh, ml = tab[2 * inverse], tab[2 * inverse + 1]
    y = dot(jnp.concatenate([hi, lo, hi], 1), jnp.concatenate([mh, mh, ml], 0))
    return y[:, :n], y[:, n:]


def left(x, tab, inverse):
    n = x[0].shape[0]
    hi, lo = split(jnp.concatenate(x, 0))
    mh, ml = tab[2 - 2 * inverse], tab[3 - 2 * inverse]
    y = dot(jnp.concatenate([mh, mh, ml], 1), jnp.concatenate([hi, lo, hi], 0))
    return y[:n], y[n:]


def side(x):
    n = x[0].shape[1]
    return tuple(jnp.concatenate([a[i : i + n] for i in range(0, a.shape[0], n)], 1) for a in x)


def stack(x):
    n = x[0].shape[0]
    return tuple(jnp.concatenate([a[:, i : i + n] for i in range(0, a.shape[1], n)], 0) for a in x)


def there_and_back(x, tab, between):
    n = x.shape[2]

    def one(inverse, _):
        y = stack(left(side(right((x[0], x[1]), tab, inverse)), tab, inverse))
        x[0], x[1] = y

        @pl.when(inverse == 0)
        def _():
            lax.fori_loop(0, x.shape[1] // n, lambda s, _: between(s), None)

    lax.fori_loop(0, 2, one, None)


def at_position(s, n):
    return pl.ds(s * n if isinstance(s, int) else pl.multiple_of(s * n, n), n)


def load(x, s):
    rows = at_position(s, x.shape[2])
    return x[0, rows], x[1, rows]


def save(x, s, value):
    rows = at_position(s, x.shape[2])
    x[0, rows], x[1, rows] = value


def cmul(a, b):
    return a[0] * b[0] - a[1] * b[1], a[0] * b[1] + a[1] * b[0]


def conj_mul(a, b):
    return a[0] * b[0] + a[1] * b[1], a[0] * b[1] - a[1] * b[0]


def iota(n, dim):
    return lax.broadcasted_iota(jnp.int32, (n, n), dim)


def slot_mask(start, core, n):
    return (1 - 2 * core) * (iota(n, 1) - start) - core < 0


def pick(mask, slot, x):
    return jnp.where(mask, x, 0.0) if slot == 0 else jnp.where(mask, 0.0, x)


def masks_of(info, offsets, sizes, j, slot, n):
    tile = info[0] - j
    tile = jnp.where(tile < 0, tile + sizes[0], tile)
    r, q = offsets[j, 2 * slot], offsets[j, 2 * slot + 1]
    i = iota(n, 0)
    upper = i >= jnp.maximum(r, jnp.where(tile == 0, n // 2, 0))
    lower = i < jnp.minimum(r, jnp.where(tile == sizes[0] - 1, n // 2, n))
    return upper, lower, slot_mask(q, info[1] % 2, n)


def gather(obj, j, masks):
    upper, lower, cols = masks
    k = (j - 1) % obj.shape[0] if isinstance(j, int) else jnp.where(j == 0, obj.shape[0], j) - 1
    return tuple(
        jnp.where(
            upper,
            jnp.where(cols, obj[j, 0, p], obj[j, 1, p]),
            jnp.where(lower, jnp.where(cols, obj[k, 0, p], obj[k, 1, p]), 0.0),
        )
        for p in range(2)
    )


def scatter(grads, masks, tiles, k, slot, p):
    total = 0.0
    for j, half in ((k, 0), ((k + 1) % tiles, 1)):
        for m in range(BATCH):
            rows = masks[j][m][half]
            total = total + pick(masks[j][m][2], slot, jnp.where(rows, grads[j][m][p], 0.0))
    return total


def emit(grads, masks, tiles, outs, last):
    for slot, out in enumerate(outs):
        for p in range(2):
            if last:
                n = out.shape[-1]
                mine = iota(n, 0) >= n // 2
                out[p] = jnp.where(
                    mine, scatter(grads, masks, tiles, 0, slot, p), scatter(grads, masks, tiles, tiles - 1, slot, p)
                )
            else:
                for k in range(tiles):
                    out[k, p] = scatter(grads, masks, tiles, k, slot, p)


def scatter_all(grads, outs, info, offsets, sizes, period):
    tiles, n = sizes[0], grads.shape[2]

    def block(k):
        total = [[0.0, 0.0], [0.0, 0.0]]
        for j, half in ((k, 0), (jnp.where(k == tiles - 1, 0, k + 1), 1)):
            for m in range(BATCH):
                masks = masks_of(info, offsets, sizes, j, period * BATCH + m, n)
                grad = load(grads, j * BATCH + m)
                for p in range(2):
                    g = jnp.where(masks[half], grad[p], 0.0)
                    for slot in range(2):
                        total[slot][p] = total[slot][p] + pick(masks[2], slot, g)
        return total

    def write(k, _):
        total = block(k)
        for slot in range(2):
            for p in range(2):
                outs[slot][k, p] = total[slot][p]

    lax.fori_loop(0, tiles, write, None)


def advance(obj_in, obj_out, sums, info, sizes, first):
    tiles, n = obj_out.shape[0], obj_out.shape[-1]
    core, j = info[1] % 2, iota(n, 1)
    low = jnp.where(jnp.logical_and(core == 0, info[1] == 0), n // 2, 0)
    high = jnp.where(jnp.logical_and(core == 1, info[1] == sizes[1] - 1), n // 2, n)

    def block(k, _):
        inside = jnp.logical_and(j >= low, j < high)
        for slot in range(2):
            own, got = sums[2 * slot], sums[2 * slot + 1]
            for p in range(2):
                s = own[k, p] + got[k, p]
                if not first:
                    s = STEP * s if slot == 0 else jnp.where(inside, STEP * s, 0.0)
                    s = obj_in[k, slot, p] - s
                obj_out[k, slot, p] = s

    lax.fori_loop(0, tiles, block, None)


def rows_of(x, tiles, n):
    at = lambda a, j, m: a[(j * BATCH + m) * n : (j * BATCH + m + 1) * n]
    return [[(at(x[0], j, m), at(x[1], j, m)) for m in range(BATCH)] for j in range(tiles)]


def stacked(parts):
    flat = [part for row in parts for part in row]
    return tuple(jnp.concatenate([part[p] for part in flat], 0) for p in range(2))


def tiled(wave, count):
    return tuple(jnp.concatenate([wave[p]] * count, 1) for p in range(2))


def kernel_a(period, sizes, first, info, offsets, *refs):
    obj_in = None if first else refs[0]
    *sums, probe, wave, tab, obj_out, inner = refs[0 if first else 1 :]
    advance(obj_in, obj_out, sums, info, sizes, first)
    n = obj_out.shape[-1]

    def enter(j, _):
        for m in range(BATCH):
            patch = gather(obj_out, j, masks_of(info, offsets, sizes, j, period * BATCH + m, n))
            save(inner, j * BATCH + m, cmul((probe[j, m, 0], probe[j, m, 1]), patch))

    lax.fori_loop(0, sizes[0], enter, None)
    there_and_back(inner, tab, lambda s: save(inner, s, cmul(load(inner, s), (wave[0], wave[1]))))


def kernel_g(period, sizes, first, tiles, info, offsets, counts, *refs):
    obj_in = None if first else refs[0]
    refs = refs[0 if first else 1 :]
    sums, inner, measured = refs[:4], refs[4], refs[5 : 5 + tiles]
    probe, wave, tab, obj_out, ge, go, he, ho, x, kept = refs[5 + tiles :]
    advance(obj_in, obj_out, sums, info, sizes, first)
    n = obj_out.shape[-1]
    count = tiles * BATCH
    for j in range(tiles):
        for m in range(BATCH):
            s = j * BATCH + m
            patch = gather(obj_out, j, masks_of(info, offsets, sizes, j, period * BATCH + m, n))
            save(kept, s, patch)
            save(x, s, cmul(load(inner, s), patch))

    def alive(j, m):
        return jnp.where(period * BATCH + m < counts[j], 1.0, 0.0)

    def exit_plane(j, _):
        for m in range(BATCH):
            s = j * BATCH + m
            wave_out, patch = load(x, s), load(kept, s)
            g = conj_mul(load(inner, s), wave_out)
            save(x, s, conj_mul(patch, wave_out))
            save(kept, s, (g[0] * alive(j, m), g[1] * alive(j, m)))

    def entrance_plane(j, _):
        for m in range(BATCH):
            s = j * BATCH + m
            g = conj_mul((probe[j, m, 0], probe[j, m, 1]), load(x, s))
            save(x, s, (g[0] * alive(j, m), g[1] * alive(j, m)))

    def there_and_back_again(turn, _):
        y = left(side(right((x[0], x[1]), tab, 0)), tab, 0)
        level = jnp.concatenate([measured[j][m] for j in range(tiles) for m in range(BATCH)], 1)
        e = y[0] * y[0] + y[1] * y[1] - level
        q = conj_mul(tiled(wave, count), y)
        z = tuple(jnp.where(turn == 0, e * y[p], q[p]) for p in range(2))
        z = right(stack(left(z, tab, 1)), tab, 1)
        x[0] = z[0]
        x[1] = z[1]

        @pl.when(turn == 0)
        def _():
            lax.fori_loop(0, tiles, exit_plane, None)
            scatter_all(kept, (he, ho), info, offsets, sizes, period)

    lax.fori_loop(0, 2, there_and_back_again, None)
    lax.fori_loop(0, tiles, entrance_plane, None)
    scatter_all(x, (ge, go), info, offsets, sizes, period)


def kernel_b(period, sizes, tiles, info, offsets, counts, obj_in, *refs):
    sums, inner, measured = refs[:4], refs[4], refs[5 : 5 + tiles]
    tab, obj_out, back, he, ho = refs[5 + tiles :]
    advance(obj_in, obj_out, sums, info, sizes, False)
    n = obj_out.shape[-1]
    masks = [[masks_of(info, offsets, sizes, j, period * BATCH + m, n) for m in range(BATCH)] for j in range(tiles)]
    seconds = [[gather(obj_out, j, masks[j][m]) for m in range(BATCH)] for j in range(tiles)]
    waves = rows_of((inner[0], inner[1]), tiles, n)
    x = stacked([[cmul(waves[j][m], seconds[j][m]) for m in range(BATCH)] for j in range(tiles)])
    x = left(side(right(x, tab, 0)), tab, 0)
    level = jnp.concatenate([measured[j][m] for j in range(tiles) for m in range(BATCH)], 1)
    e = x[0] * x[0] + x[1] * x[1] - level
    x = right(stack(left((e * x[0], e * x[1]), tab, 1)), tab, 1)
    exits = rows_of(x, tiles, n)
    x = stacked([[conj_mul(seconds[j][m], exits[j][m]) for m in range(BATCH)] for j in range(tiles)])
    back[0] = x[0]
    back[1] = x[1]
    emit(live_grads(waves, exits, counts, period), masks, tiles, (he, ho), True)


def live_grads(forward, backward, counts, period):
    grads = []
    for j, row in enumerate(forward):
        grads.append([])
        for m, wave in enumerate(row):
            live = jnp.where(period * BATCH + m < counts[j], 1.0, 0.0)
            g = conj_mul(wave, backward[j][m])
            grads[j].append((g[0] * live, g[1] * live))
    return grads


def kernel_c(period, sizes, info, offsets, counts, back, probe, wave, tab, ge, go):
    tiles, n = probe.shape[0], probe.shape[-1]
    masks = [[masks_of(info, offsets, sizes, j, period * BATCH + m, n) for m in range(BATCH)] for j in range(tiles)]
    x = left(side(right((back[0], back[1]), tab, 0)), tab, 0)
    x = left(conj_mul(tiled(wave, tiles * BATCH), x), tab, 1)
    waves = rows_of(right(stack(x), tab, 1), tiles, n)
    probes = [[(probe[j, m, 0], probe[j, m, 1]) for m in range(BATCH)] for j in range(tiles)]
    emit(live_grads(probes, waves, counts, period), masks, tiles, (ge, go), True)


def kernel_roll(period, offsets, probe, out):
    tiles, n = out.shape[0], out.shape[-1]

    def one(j, _):
        for m in range(BATCH):
            r = lax.rem(offsets[j, 2 * (period * BATCH + m)], n)
            q = lax.rem(offsets[j, 2 * (period * BATCH + m) + 1], n)
            for p in range(2):
                out[j, m, p] = pltpu.roll(pltpu.roll(probe[p], r, 0), q, 1)

    lax.fori_loop(0, tiles, one, None)


def kernel_place(info, *refs):
    *tiles, pe, po = refs
    n = pe.shape[-1]
    cols = slot_mask(n // 2, info[1] % 2, n)
    mine = iota(n, 0) >= n // 2
    for p in range(2):
        rolled = [pltpu.roll(pltpu.roll(tile[p], n // 2, 0), n // 2, 1) for tile in tiles]
        for k in range(len(tiles)):
            x = jnp.where(mine, rolled[k], rolled[(k + 1) % len(tiles)])
            pe[k, p] = pick(cols, 0, x)
            po[k, p] = pick(cols, 1, x)


def kernel_end(info, obj, fe, re, fo, ro, out):
    tiles, n = obj.shape[0], obj.shape[-1]
    cols = slot_mask(n // 2, info[1] % 2, n)
    mine = iota(n, 0) >= n // 2
    for p in range(2):
        x = [jnp.where(mine, obj[0, slot, p], obj[tiles - 1, slot, p]) for slot in range(2)]
        x = jnp.where(cols, x[0] - STEP * (fe[p] + re[p]), x[1] - STEP * (fo[p] + ro[p]))
        out[p] = pltpu.roll(pltpu.roll(x, n // 2, 0), n // 2, 1)


def call(kernel, scalars, arrays, outs, scratch=()):
    return pl.pallas_call(
        kernel,
        out_shape=[jax.ShapeDtypeStruct(s, F32) for s in outs],
        in_specs=[pl.BlockSpec(memory_space=pltpu.SMEM)] * len(scalars)
        + [pl.BlockSpec(memory_space=pltpu.VMEM)] * len(arrays),
        out_specs=[pl.BlockSpec(memory_space=pltpu.VMEM)] * len(outs),
        scratch_shapes=[pltpu.VMEM(x, F32) for x in scratch],
        compiler_params=pltpu.CompilerParams(vmem_limit_bytes=24 * 1024 * 1024),
    )(*scalars, *arrays)


def local(object_field, probe, propagator, offsets, counts, intensity):
    n = probe.shape[1]
    sizes = (lax.axis_size("gx"), lax.axis_size("gy"))
    tiles = sizes[0]
    slots = offsets.shape[2]
    ay = lax.axis_index("gy")
    chips = sizes[1] // 2
    chip = ay // 2
    chip = jnp.where(2 * chip < chips, chip, chips // 2 + chips - 1 - chip)
    info = jnp.stack([lax.axis_index("gx"), 2 * chip + ay % 2]).astype(jnp.int32)
    meta = jnp.concatenate([offsets.reshape(-1), counts.reshape(-1)]).astype(F32)
    meta = jnp.pad(meta, (0, n - meta.shape[0])).reshape(1, n)
    meta = jnp.broadcast_to(meta, (8, n))

    own = place_tiles(jnp.concatenate([object_field[0].reshape(2 * n, n), meta]))
    own1 = place_tiles(jnp.concatenate([object_field[1], intensity[0, 0, :BATCH]]))
    own1, own2 = own1[:2], own1[2:]
    packed = column(own)
    own3 = place_tiles(intensity[0, 0, BATCH:])
    tiles1 = column(own1)
    measured = [column(own2)]
    tiles0 = [x[: 2 * n].reshape(2, n, n) for x in packed]
    meta = jnp.stack([x[2 * n, : 2 * slots + 1] for x in packed]).astype(jnp.int32)
    offs, count = meta[:, : 2 * slots], meta[:, 2 * slots]
    tab = dft_tables(n)
    wave = jnp.stack([jnp.cos(propagator), jnp.sin(propagator)])
    pair, state = (2, n, n), (tiles, 2, 2, n, n)
    half, waves = (tiles, 2, n, n), (2, tiles * BATCH * n, n)

    def roll(b):
        return call(functools.partial(kernel_roll, b), [offs], [probe], [(tiles, 2, 2, n, n)])[0]

    def start(parts):
        pe, po = call(kernel_place, [info], parts, [half] * 2)
        ro = swap_cols(po)
        return [pe, swap_core(pe), po, ro]

    sums0 = start(tiles0)
    sums1 = start(tiles1)
    measured.append(column(own3[:BATCH]))
    probes = [roll(0)]
    obj0, obj1 = [], []
    for b in range(NB):
        first, last = b == 0, b == NB - 1
        out0, inner = call(
            functools.partial(kernel_a, b, sizes, first), [info, offs],
            [*obj0, *sums0, probes[b], wave, tab], [state, waves],
        )
        if last:
            break
        out1, ge, go, he, ho = call(
            functools.partial(kernel_g, b, sizes, first, tiles), [info, offs, count],
            [*obj1, *sums1, inner, *measured[b], probes[b], wave, tab], [state, half, half, half, half], [waves, waves],
        )
        obj0, obj1 = [out0], [out1]
        ro = swap_cols(go)
        sums0 = [ge, swap_core(ge), go, ro]
        ro = swap_cols(ho)
        sums1 = [he, swap_core(he), ho, ro]
        probes.append(roll(b + 1))
        if b + 2 < NB:
            measured.append(column(own3[(b + 1) * BATCH : (b + 2) * BATCH]))
    b = NB - 1
    out1, back, he, ho = call(
        functools.partial(kernel_b, b, sizes, tiles), [info, offs, count],
        [*obj1, *sums1, inner, *measured[b], tab], [state, waves, pair, pair],
    )
    sums1 = [he, swap_core(he), ho, swap_cols(ho)]
    ge, go = call(
        functools.partial(kernel_c, b, sizes), [info, offs, count],
        [back, probes[b], wave, tab], [pair, pair],
    )
    sums0 = [ge, swap_core(ge), go, swap_cols(go)]
    (last1,) = call(kernel_end, [info], [out1, *sums1], [pair])
    (last0,) = call(kernel_end, [info], [out0, *sums0], [pair])
    last1 = place_tiles(last1)
    last0 = place_tiles(last0)
    return jnp.stack([last0, last1])


def solution(mesh):
    in_specs = (
        P(None, None, "gx", "gy"),
        P(),
        P(),
        P("gx", "gy", None, None),
        P("gx", "gy"),
        P("gx", "gy", None, None, None),
    )
    out_specs = P(None, None, "gx", "gy")
    return jax.shard_map(local, mesh=mesh, in_specs=in_specs, out_specs=out_specs, check_vma=False)
```

profile of v0, /device:TPU:12, one launch (start us, length us, event | category | flops | bytes accessed | tf_op | source)
XLA Modules:
  0.0 236.2 jit_solution(18085887860633283857)
XLA Ops:
  1.9 3.4 %collective-permute-start.6 = (f32[4,128,128]{2,1,0:T(8,128)S(1)}, f32[4,128,128]{2,1,0:T(8,128)S(1)}, u32[]{:S(2)}, u32[]{:S(2)}) collective-permute-start(f32[4,128,128]{2,1,0:T(8,128)S(1)} %pad_maximum_fusion), channel_id=1, source_target_pairs={{0,0},{1,1},{2,2},{3,3},{4,6},{5,7},{6,4},{7,5},{8,8},{9,9},{10,10... | collective-permute-start | bytes 786440 | tf_op jit(solution)/shard_map/ppermute | solution.py:41
  8.8 6.0 %collective-permute-done = f32[264,128]{1,0:T(8,128)S(1)} collective-permute-done((f32[264,128]{1,0:T(8,128)S(1)}, f32[264,128]{1,0:T(8,128)S(1)}, u32[]{:S(2)}, u32[]{:S(2)}) %collective-permute-start) | collective-permute-done | bytes 135200 | tf_op jit(solution)/shard_map/ppermute | solution.py:41
  19.8 3.6 %collective-permute-start.8 = (f32[2,128,128]{2,1,0:T(8,128)S(1)}, f32[2,128,128]{2,1,0:T(8,128)S(1)}, u32[]{:S(2)}, u32[]{:S(2)}) collective-permute-start(f32[2,128,128]{2,1,0:T(8,128)S(1)} %get-tuple-element.105.refs_0_), channel_id=1, source_target_pairs={{0,16},{8,24},{16,0},{24,8},{1,17},{9,25},{17,1},{25,9},{2,18},{10... | collective-permute-start | bytes 393224 | tf_op jit(solution)/shard_map/ppermute | solution.py:48
  26.0 8.5 %collective-permute-done.2 = f32[264,128]{1,0:T(8,128)S(1)} collective-permute-done((f32[264,128]{1,0:T(8,128)S(1)}, f32[264,128]{1,0:T(8,128)S(1)}, u32[]{:S(2)}, u32[]{:S(2)}) %collective-permute-start.2) | collective-permute-done | bytes 135200 | tf_op jit(solution)/shard_map/ppermute | solution.py:48
  44.0 3.1 %collective-permute-start.11 = (f32[4,2,128,128]{3,2,1,0:T(8,128)S(1)}, f32[4,2,128,128]{3,2,1,0:T(8,128)S(1)}, u32[]{:S(2)}, u32[]{:S(2)}) collective-permute-start(f32[4,2,128,128]{3,2,1,0:T(8,128)S(1)} %get-tuple-element.56.refs_2_), channel_id=1, source_target_pairs={{1,2},{2,1},{3,6},{6,3},{7,4},{4,7},{9,10},{10,9},{11,14},{14,11},... | collective-permute-start | bytes 1572872 | tf_op jit(solution)/shard_map/ppermute | solution.py:36
  47.5 2.8 %collective-permute-start.13 = (f32[2,128,128]{2,1,0:T(8,128)S(1)}, f32[2,128,128]{2,1,0:T(8,128)S(1)}, u32[]{:S(2)}, u32[]{:S(2)}) collective-permute-start(f32[2,128,128]{2,1,0:T(8,128)S(1)} %get-tuple-element.104.refs_5_), channel_id=1, source_target_pairs={{0,16},{8,24},{16,0},{24,8},{1,17},{9,25},{17,1},{25,9},{2,18},{10... | collective-permute-start | bytes 393224 | tf_op jit(solution)/shard_map/ppermute | solution.py:48
  53.1 4.7 %shard_map.102 = (f32[4,2,2,128,128]{4,3,2,1,0:T(8,128)S(1)}, f32[2,1024,128]{2,1,0:T(8,128)S(1)}) custom-call(s32[2]{0:T(128)S(1)} %pad_add_fusion.info, s32[4,24]{1,0:T(4,128)S(1)} %bitcast.23, f32[4,2,128,128]{3,2,1,0:T(8,128)S(1)} %get-tuple-element.52.refs_0_, f32[4,2,128,128]{3,2,1,0:T(8,128)S(1)} %collective-permute-done.4.refs_1_, ...), custom_call_target="tpu_custom_call" | custom-call | tf_op jit(solution)/shard_map/pallas_call | solution.py:399
  57.8 9.8 %collective-permute-done.11.refs_3_ = f32[4,2,128,128]{3,2,1,0:T(8,128)S(1)} collective-permute-done((f32[4,2,128,128]{3,2,1,0:T(8,128)S(1)}, f32[4,2,128,128]{3,2,1,0:T(8,128)S(1)}, u32[]{:S(2)}, u32[]{:S(2)}) %collective-permute-start.11) | collective-permute-done | bytes 524320 | tf_op jit(solution)/shard_map/ppermute | solution.py:36
  67.6 8.1 %shard_map.104 = (f32[4,2,2,128,128]{4,3,2,1,0:T(8,128)S(1)}, f32[4,2,128,128]{3,2,1,0:T(8,128)S(1)}, f32[4,2,128,128]{3,2,1,0:T(8,128)S(1)}, f32[4,2,128,128]{3,2,1,0:T(8,128)S(1)}, f32[4,2,128,128]{3,2,1,0:T(8,128)S(1)}) custom-call(s32[2]{0:T(128)S(1)} %pad_add_fusion.info, s32[4,24]{1,0:T(4,128)S(1)} %bitcast.24, s32[4]{0:T(128)S(1)} %slice_reduce_fusion.counts, ...), custom_call_target="tpu_custom_call" | custom-call | tf_op jit(solution)/shard_map/pallas_call | solution.py:399
  87.4 4.8 %shard_map.106 = (f32[4,2,2,128,128]{4,3,2,1,0:T(8,128)S(1)}, f32[2,1024,128]{2,1,0:T(8,128)S(1)}) custom-call(s32[2]{0:T(128)S(1)} %pad_add_fusion.info, s32[4,24]{1,0:T(4,128)S(1)} %bitcast.26, f32[4,2,2,128,128]{4,3,2,1,0:T(8,128)S(1)} %get-tuple-element.54.refs_0_, f32[4,2,128,128]{3,2,1,0:T(8,128)S(1)} %get-tuple-element.58.refs_1_, ...), custom_call_target="tpu_custom_call" | custom-call | tf_op jit(solution)/shard_map/pallas_call | solution.py:399
  94.8 8.1 %shard_map.107 = (f32[4,2,2,128,128]{4,3,2,1,0:T(8,128)S(1)}, f32[4,2,128,128]{3,2,1,0:T(8,128)S(1)}, f32[4,2,128,128]{3,2,1,0:T(8,128)S(1)}, f32[4,2,128,128]{3,2,1,0:T(8,128)S(1)}, f32[4,2,128,128]{3,2,1,0:T(8,128)S(1)}) custom-call(s32[2]{0:T(128)S(1)} %pad_add_fusion.info, s32[4,24]{1,0:T(4,128)S(1)} %bitcast.27, s32[4]{0:T(128)S(1)} %slice_reduce_fusion.counts, ...), custom_call_target="tpu_custom_call" | custom-call | tf_op jit(solution)/shard_map/pallas_call | solution.py:399
  103.0 4.9 %collective-permute-start.24 = (f32[4,2,128,128]{3,2,1,0:T(8,128)S(1)}, f32[4,2,128,128]{3,2,1,0:T(8,128)S(1)}, u32[]{:S(2)}, u32[]{:S(2)}) collective-permute-start(f32[4,2,128,128]{3,2,1,0:T(8,128)S(1)} %get-tuple-element.66.refs_3_), channel_id=1, source_target_pairs={{1,2},{2,1},{3,6},{6,3},{7,4},{4,7},{9,10},{10,9},{11,14},{14,11},... | collective-permute-start | bytes 1572872 | tf_op jit(solution)/shard_map/ppermute | solution.py:36
  110.6 3.1 %collective-permute-start.28 = (f32[2,128,128]{2,1,0:T(8,128)S(1)}, f32[2,128,128]{2,1,0:T(8,128)S(1)}, u32[]{:S(2)}, u32[]{:S(2)}) collective-permute-start(f32[2,128,128]{2,1,0:T(8,128)S(1)} %get-tuple-element.102.refs_6_), channel_id=1, source_target_pairs={{0,16},{8,24},{16,0},{24,8},{1,17},{9,25},{17,1},{25,9},{2,18},{10... | collective-permute-start | bytes 393224 | tf_op jit(solution)/shard_map/ppermute | solution.py:48
  116.8 4.8 %shard_map.109 = (f32[4,2,2,128,128]{4,3,2,1,0:T(8,128)S(1)}, f32[2,1024,128]{2,1,0:T(8,128)S(1)}) custom-call(s32[2]{0:T(128)S(1)} %pad_add_fusion.info, s32[4,24]{1,0:T(4,128)S(1)} %bitcast.29, f32[4,2,2,128,128]{4,3,2,1,0:T(8,128)S(1)} %get-tuple-element.60.refs_0_, f32[4,2,128,128]{3,2,1,0:T(8,128)S(1)} %get-tuple-element.65.refs_1_, ...), custom_call_target="tpu_custom_call" | custom-call | tf_op jit(solution)/shard_map/pallas_call | solution.py:399
  124.0 8.2 %shard_map.110 = (f32[4,2,2,128,128]{4,3,2,1,0:T(8,128)S(1)}, f32[4,2,128,128]{3,2,1,0:T(8,128)S(1)}, f32[4,2,128,128]{3,2,1,0:T(8,128)S(1)}, f32[4,2,128,128]{3,2,1,0:T(8,128)S(1)}, f32[4,2,128,128]{3,2,1,0:T(8,128)S(1)}) custom-call(s32[2]{0:T(128)S(1)} %pad_add_fusion.info, s32[4,24]{1,0:T(4,128)S(1)} %bitcast.30, s32[4]{0:T(128)S(1)} %slice_reduce_fusion.counts, ...), custom_call_target="tpu_custom_call" | custom-call | tf_op jit(solution)/shard_map/pallas_call | solution.py:399
  132.3 4.8 %collective-permute-start.31 = (f32[4,2,128,128]{3,2,1,0:T(8,128)S(1)}, f32[4,2,128,128]{3,2,1,0:T(8,128)S(1)}, u32[]{:S(2)}, u32[]{:S(2)}) collective-permute-start(f32[4,2,128,128]{3,2,1,0:T(8,128)S(1)} %get-tuple-element.73.refs_3_), channel_id=1, source_target_pairs={{1,2},{2,1},{3,6},{6,3},{7,4},{4,7},{9,10},{10,9},{11,14},{14,11},... | collective-permute-start | bytes 1572872 | tf_op jit(solution)/shard_map/ppermute | solution.py:36
  137.2 2.9 %collective-permute-start.33 = (f32[4,2,128,128]{3,2,1,0:T(8,128)S(1)}, f32[4,2,128,128]{3,2,1,0:T(8,128)S(1)}, u32[]{:S(2)}, u32[]{:S(2)}) collective-permute-start(f32[4,2,128,128]{3,2,1,0:T(8,128)S(1)} %get-tuple-element.77.refs_3_), channel_id=1, source_target_pairs={{1,2},{2,1},{3,6},{6,3},{7,4},{4,7},{9,10},{10,9},{11,14},{14,11},... | collective-permute-start | bytes 1572872 | tf_op jit(solution)/shard_map/ppermute | solution.py:36
  145.1 4.8 %shard_map.112 = (f32[4,2,2,128,128]{4,3,2,1,0:T(8,128)S(1)}, f32[2,1024,128]{2,1,0:T(8,128)S(1)}) custom-call(s32[2]{0:T(128)S(1)} %pad_add_fusion.info, s32[4,24]{1,0:T(4,128)S(1)} %bitcast.32, f32[4,2,2,128,128]{4,3,2,1,0:T(8,128)S(1)} %get-tuple-element.67.refs_0_, f32[4,2,128,128]{3,2,1,0:T(8,128)S(1)} %get-tuple-element.72.refs_1_, ...), custom_call_target="tpu_custom_call" | custom-call | tf_op jit(solution)/shard_map/pallas_call | solution.py:399
  152.2 8.2 %shard_map.113 = (f32[4,2,2,128,128]{4,3,2,1,0:T(8,128)S(1)}, f32[4,2,128,128]{3,2,1,0:T(8,128)S(1)}, f32[4,2,128,128]{3,2,1,0:T(8,128)S(1)}, f32[4,2,128,128]{3,2,1,0:T(8,128)S(1)}, f32[4,2,128,128]{3,2,1,0:T(8,128)S(1)}) custom-call(s32[2]{0:T(128)S(1)} %pad_add_fusion.info, s32[4,24]{1,0:T(4,128)S(1)} %bitcast.33, s32[4]{0:T(128)S(1)} %slice_reduce_fusion.counts, ...), custom_call_target="tpu_custom_call" | custom-call | tf_op jit(solution)/shard_map/pallas_call | solution.py:399
  160.5 4.9 %collective-permute-start.38 = (f32[4,2,128,128]{3,2,1,0:T(8,128)S(1)}, f32[4,2,128,128]{3,2,1,0:T(8,128)S(1)}, u32[]{:S(2)}, u32[]{:S(2)}) collective-permute-start(f32[4,2,128,128]{3,2,1,0:T(8,128)S(1)} %get-tuple-element.80.refs_3_), channel_id=1, source_target_pairs={{1,2},{2,1},{3,6},{6,3},{7,4},{4,7},{9,10},{10,9},{11,14},{14,11},... | collective-permute-start | bytes 1572872 | tf_op jit(solution)/shard_map/ppermute | solution.py:36
  165.5 3.0 %collective-permute-start.40 = (f32[4,2,128,128]{3,2,1,0:T(8,128)S(1)}, f32[4,2,128,128]{3,2,1,0:T(8,128)S(1)}, u32[]{:S(2)}, u32[]{:S(2)}) collective-permute-start(f32[4,2,128,128]{3,2,1,0:T(8,128)S(1)} %get-tuple-element.84.refs_3_), channel_id=1, source_target_pairs={{1,2},{2,1},{3,6},{6,3},{7,4},{4,7},{9,10},{10,9},{11,14},{14,11},... | collective-permute-start | bytes 1572872 | tf_op jit(solution)/shard_map/ppermute | solution.py:36
  173.4 4.8 %shard_map.115 = (f32[4,2,2,128,128]{4,3,2,1,0:T(8,128)S(1)}, f32[2,1024,128]{2,1,0:T(8,128)S(1)}) custom-call(s32[2]{0:T(128)S(1)} %pad_add_fusion.info, s32[4,24]{1,0:T(4,128)S(1)} %bitcast.35, f32[4,2,2,128,128]{4,3,2,1,0:T(8,128)S(1)} %get-tuple-element.74.refs_0_, f32[4,2,128,128]{3,2,1,0:T(8,128)S(1)} %get-tuple-element.79.refs_1_, ...), custom_call_target="tpu_custom_call" | custom-call | tf_op jit(solution)/shard_map/pallas_call | solution.py:399
  180.5 8.2 %shard_map.116 = (f32[4,2,2,128,128]{4,3,2,1,0:T(8,128)S(1)}, f32[4,2,128,128]{3,2,1,0:T(8,128)S(1)}, f32[4,2,128,128]{3,2,1,0:T(8,128)S(1)}, f32[4,2,128,128]{3,2,1,0:T(8,128)S(1)}, f32[4,2,128,128]{3,2,1,0:T(8,128)S(1)}) custom-call(s32[2]{0:T(128)S(1)} %pad_add_fusion.info, s32[4,24]{1,0:T(4,128)S(1)} %bitcast.36, s32[4]{0:T(128)S(1)} %slice_reduce_fusion.counts, ...), custom_call_target="tpu_custom_call" | custom-call | tf_op jit(solution)/shard_map/pallas_call | solution.py:399
  188.8 4.9 %collective-permute-start.45 = (f32[4,2,128,128]{3,2,1,0:T(8,128)S(1)}, f32[4,2,128,128]{3,2,1,0:T(8,128)S(1)}, u32[]{:S(2)}, u32[]{:S(2)}) collective-permute-start(f32[4,2,128,128]{3,2,1,0:T(8,128)S(1)} %get-tuple-element.87.refs_3_), channel_id=1, source_target_pairs={{1,2},{2,1},{3,6},{6,3},{7,4},{4,7},{9,10},{10,9},{11,14},{14,11},... | collective-permute-start | bytes 1572872 | tf_op jit(solution)/shard_map/ppermute | solution.py:36
  193.8 2.9 %collective-permute-start.47 = (f32[4,2,128,128]{3,2,1,0:T(8,128)S(1)}, f32[4,2,128,128]{3,2,1,0:T(8,128)S(1)}, u32[]{:S(2)}, u32[]{:S(2)}) collective-permute-start(f32[4,2,128,128]{3,2,1,0:T(8,128)S(1)} %get-tuple-element.91.refs_2_), channel_id=1, source_target_pairs={{1,2},{2,1},{3,6},{6,3},{7,4},{4,7},{9,10},{10,9},{11,14},{14,11},... | collective-permute-start | bytes 1572872 | tf_op jit(solution)/shard_map/ppermute | solution.py:36
  201.8 4.8 %shard_map.118 = (f32[4,2,2,128,128]{4,3,2,1,0:T(8,128)S(1)}, f32[2,1024,128]{2,1,0:T(8,128)S(1)}) custom-call(s32[2]{0:T(128)S(1)} %pad_add_fusion.info, s32[4,24]{1,0:T(4,128)S(1)} %bitcast.38, f32[4,2,2,128,128]{4,3,2,1,0:T(8,128)S(1)} %get-tuple-element.81.refs_0_, f32[4,2,128,128]{3,2,1,0:T(8,128)S(1)} %get-tuple-element.86.refs_1_, ...), custom_call_target="tpu_custom_call" | custom-call | tf_op jit(solution)/shard_map/pallas_call | solution.py:399
  208.7 3.5 %shard_map.119 = (f32[4,2,2,128,128]{4,3,2,1,0:T(8,128)S(1)}, f32[2,1024,128]{2,1,0:T(8,128)S(1)}, f32[2,128,128]{2,1,0:T(8,128)S(1)}, f32[2,128,128]{2,1,0:T(8,128)S(1)}) custom-call(s32[2]{0:T(128)S(1)} %pad_add_fusion.info, s32[4,24]{1,0:T(4,128)S(1)} %bitcast.39, s32[4]{0:T(128)S(1)} %slice_reduce_fusion.counts, ...), custom_call_target="tpu_custom_call" | custom-call | tf_op jit(solution)/shard_map/pallas_call | solution.py:399
  212.2 3.2 %shard_map.120 = (f32[2,128,128]{2,1,0:T(8,128)S(1)}, f32[2,128,128]{2,1,0:T(8,128)S(1)}) custom-call(s32[2]{0:T(128)S(1)} %pad_add_fusion.info, s32[4,24]{1,0:T(4,128)S(1)} %bitcast.40, s32[4]{0:T(128)S(1)} %slice_reduce_fusion.counts, f32[2,1024,128]{2,1,0:T(8,128)S(1)} %get-tuple-element.93.back, f32[4,2,2,128,128]{4,3,2,1,0:T(8,128)S(1)} %shard_map.117.refs_5_.probe, ...), custom_call_target="tpu_custom_call" | custom-call | tf_op jit(solution)/shard_map/pallas_call | solution.py:399
  215.5 4.9 %collective-permute-start.52 = (f32[2,128,128]{2,1,0:T(8,128)S(1)}, f32[2,128,128]{2,1,0:T(8,128)S(1)}, u32[]{:S(2)}, u32[]{:S(2)}) collective-permute-start(f32[2,128,128]{2,1,0:T(8,128)S(1)} %get-tuple-element.95.fo), channel_id=1, source_target_pairs={{1,2},{2,1},{3,6},{6,3},{7,4},{4,7},{9,10},{10,9},{11,14},{14,11},... | collective-permute-start | bytes 393224 | tf_op jit(solution)/shard_map/ppermute | solution.py:36
  220.5 3.0 %collective-permute-start.55 = (f32[2,128,128]{2,1,0:T(8,128)S(1)}, f32[2,128,128]{2,1,0:T(8,128)S(1)}, u32[]{:S(2)}, u32[]{:S(2)}) collective-permute-start(f32[2,128,128]{2,1,0:T(8,128)S(1)} %get-tuple-element.98.fo), channel_id=1, source_target_pairs={{1,2},{2,1},{3,6},{6,3},{7,4},{4,7},{9,10},{10,9},{11,14},{14,11},... | collective-permute-start | bytes 393224 | tf_op jit(solution)/shard_map/ppermute | solution.py:36
  224.1 3.1 %collective-permute-start.53 = (f32[2,128,128]{2,1,0:T(8,128)S(1)}, f32[2,128,128]{2,1,0:T(8,128)S(1)}, u32[]{:S(2)}, u32[]{:S(2)}) collective-permute-start(f32[2,128,128]{2,1,0:T(8,128)S(1)} %shard_map.121), channel_id=1, source_target_pairs={{0,0},{1,1},{2,2},{3,3},{4,6},{5,7},{6,4},{7,5},{8,8},{9,9},{10,10... | collective-permute-start | bytes 393224 | tf_op jit(solution)/shard_map/ppermute | solution.py:41
  231.4 4.0 %collective-permute-done.56 = f32[2,128,128]{2,1,0:T(8,128)S(1)} collective-permute-done((f32[2,128,128]{2,1,0:T(8,128)S(1)}, f32[2,128,128]{2,1,0:T(8,128)S(1)}, u32[]{:S(2)}, u32[]{:S(2)}) %collective-permute-start.56) | collective-permute-done | bytes 131104 | tf_op jit(solution)/shard_map/ppermute | solution.py:41
  (141 shorter events, 75.0 us)
Async XLA Ops:
  1.9 17.5 %collective-permute-start.6 = (f32[4,128,128]{2,1,0:T(8,128)S(1)}, f32[4,128,128]{2,1,0:T(8,128)S(1)}, u32[]{:S(2)}, u32[]{:S(2)}) collective-permute-start(f32[4,128,128]{2,1,0:T(8,128)S(1)} %pad_maximum_fusion), channel_id=1, source_target_pairs={{0,0},{1,1},{2,2},{3,3},{4,6},{5,7},{6,4},{7,5},{8,8},{9,9},{10,10... | collective-permute-start | bytes 786440 | tf_op jit(solution)/shard_map/ppermute | solution.py:41
  14.8 11.2 %collective-permute-start.1 = (f32[264,128]{1,0:T(8,128)S(1)}, f32[264,128]{1,0:T(8,128)S(1)}, u32[]{:S(2)}, u32[]{:S(2)}) collective-permute-start(f32[264,128]{1,0:T(8,128)S(1)} %collective-permute-done), channel_id=1, source_target_pairs={{0,8},{8,16},{16,24},{24,0},{1,9},{9,17},{17,25},{25,1},{2,10},{10... | collective-permute-start | bytes 405512 | tf_op jit(solution)/shard_map/ppermute | solution.py:48
  16.4 18.1 %collective-permute-start.2 = (f32[264,128]{1,0:T(8,128)S(1)}, f32[264,128]{1,0:T(8,128)S(1)}, u32[]{:S(2)}, u32[]{:S(2)}) collective-permute-start(f32[264,128]{1,0:T(8,128)S(1)} %collective-permute-done), channel_id=1, source_target_pairs={{0,16},{8,24},{16,0},{24,8},{1,17},{9,25},{17,1},{25,9},{2,18},{10... | collective-permute-start | bytes 405512 | tf_op jit(solution)/shard_map/ppermute | solution.py:48
  17.6 18.3 %collective-permute-start.3 = (f32[264,128]{1,0:T(8,128)S(1)}, f32[264,128]{1,0:T(8,128)S(1)}, u32[]{:S(2)}, u32[]{:S(2)}) collective-permute-start(f32[264,128]{1,0:T(8,128)S(1)} %collective-permute-done), channel_id=1, source_target_pairs={{0,24},{8,0},{16,8},{24,16},{1,25},{9,1},{17,9},{25,17},{2,26},{10... | collective-permute-start | bytes 405512 | tf_op jit(solution)/shard_map/ppermute | solution.py:48
  19.4 18.0 %collective-permute-start.7 = (f32[2,128,128]{2,1,0:T(8,128)S(1)}, f32[2,128,128]{2,1,0:T(8,128)S(1)}, u32[]{:S(2)}, u32[]{:S(2)}) collective-permute-start(f32[2,128,128]{2,1,0:T(8,128)S(1)} %get-tuple-element.105.refs_0_), channel_id=1, source_target_pairs={{0,8},{8,16},{16,24},{24,0},{1,9},{9,17},{17,25},{25,1},{2,10},{10... | collective-permute-start | bytes 393224 | tf_op jit(solution)/shard_map/ppermute | solution.py:48
  19.8 20.5 %collective-permute-start.8 = (f32[2,128,128]{2,1,0:T(8,128)S(1)}, f32[2,128,128]{2,1,0:T(8,128)S(1)}, u32[]{:S(2)}, u32[]{:S(2)}) collective-permute-start(f32[2,128,128]{2,1,0:T(8,128)S(1)} %get-tuple-element.105.refs_0_), channel_id=1, source_target_pairs={{0,16},{8,24},{16,0},{24,8},{1,17},{9,25},{17,1},{25,9},{2,18},{10... | collective-permute-start | bytes 393224 | tf_op jit(solution)/shard_map/ppermute | solution.py:48
  26.0 17.1 %collective-permute-start.9 = (f32[2,128,128]{2,1,0:T(8,128)S(1)}, f32[2,128,128]{2,1,0:T(8,128)S(1)}, u32[]{:S(2)}, u32[]{:S(2)}) collective-permute-start(f32[2,128,128]{2,1,0:T(8,128)S(1)} %get-tuple-element.105.refs_0_), channel_id=1, source_target_pairs={{0,24},{8,0},{16,8},{24,16},{1,25},{9,1},{17,9},{25,17},{2,26},{10... | collective-permute-start | bytes 393224 | tf_op jit(solution)/shard_map/ppermute | solution.py:48
  36.7 10.8 %collective-permute-start.4 = (f32[4,2,128,128]{3,2,1,0:T(8,128)S(1)}, f32[4,2,128,128]{3,2,1,0:T(8,128)S(1)}, u32[]{:S(2)}, u32[]{:S(2)}) collective-permute-start(f32[4,2,128,128]{3,2,1,0:T(8,128)S(1)} %get-tuple-element.52.refs_0_), channel_id=1, source_target_pairs={{0,1},{1,0},{2,3},{3,2},{4,5},{5,4},{6,7},{7,6},{8,9},{9,8},{10,11... | collective-permute-start | bytes 1572872 | tf_op jit(solution)/shard_map/ppermute | solution.py:31
  37.5 12.9 %collective-permute-start.5 = (f32[4,2,128,128]{3,2,1,0:T(8,128)S(1)}, f32[4,2,128,128]{3,2,1,0:T(8,128)S(1)}, u32[]{:S(2)}, u32[]{:S(2)}) collective-permute-start(f32[4,2,128,128]{3,2,1,0:T(8,128)S(1)} %get-tuple-element.53.refs_2_), channel_id=1, source_target_pairs={{1,2},{2,1},{3,6},{6,3},{7,4},{4,7},{9,10},{10,9},{11,14},{14,11},... | collective-permute-start | bytes 1572872 | tf_op jit(solution)/shard_map/ppermute | solution.py:36
  40.3 41.1 %collective-permute-start.19 = (f32[10,128,128]{2,1,0:T(8,128)S(1)}, f32[10,128,128]{2,1,0:T(8,128)S(1)}, u32[]{:S(2)}, u32[]{:S(2)}) collective-permute-start(f32[10,128,128]{2,1,0:T(8,128)S(1)} %slice_bitcast_fusion), channel_id=1, source_target_pairs={{0,0},{1,1},{2,2},{3,3},{4,6},{5,7},{6,4},{7,5},{8,8},{9,9},{10,10... | collective-permute-start | bytes 1966088 | tf_op jit(solution)/shard_map/ppermute | solution.py:41
  43.8 14.0 %collective-permute-start.10 = (f32[4,2,128,128]{3,2,1,0:T(8,128)S(1)}, f32[4,2,128,128]{3,2,1,0:T(8,128)S(1)}, u32[]{:S(2)}, u32[]{:S(2)}) collective-permute-start(f32[4,2,128,128]{3,2,1,0:T(8,128)S(1)} %get-tuple-element.55.refs_0_), channel_id=1, source_target_pairs={{0,1},{1,0},{2,3},{3,2},{4,5},{5,4},{6,7},{7,6},{8,9},{9,8},{10,11... | collective-permute-start | bytes 1572872 | tf_op jit(solution)/shard_map/ppermute | solution.py:31
  44.0 23.6 %collective-permute-start.11 = (f32[4,2,128,128]{3,2,1,0:T(8,128)S(1)}, f32[4,2,128,128]{3,2,1,0:T(8,128)S(1)}, u32[]{:S(2)}, u32[]{:S(2)}) collective-permute-start(f32[4,2,128,128]{3,2,1,0:T(8,128)S(1)} %get-tuple-element.56.refs_2_), channel_id=1, source_target_pairs={{1,2},{2,1},{3,6},{6,3},{7,4},{4,7},{9,10},{10,9},{11,14},{14,11},... | collective-permute-start | bytes 1572872 | tf_op jit(solution)/shard_map/ppermute | solution.py:36
  47.5 10.3 %collective-permute-start.13 = (f32[2,128,128]{2,1,0:T(8,128)S(1)}, f32[2,128,128]{2,1,0:T(8,128)S(1)}, u32[]{:S(2)}, u32[]{:S(2)}) collective-permute-start(f32[2,128,128]{2,1,0:T(8,128)S(1)} %get-tuple-element.104.refs_5_), channel_id=1, source_target_pairs={{0,16},{8,24},{16,0},{24,8},{1,17},{9,25},{17,1},{25,9},{2,18},{10... | collective-permute-start | bytes 393224 | tf_op jit(solution)/shard_map/ppermute | solution.py:48
  75.8 10.5 %collective-permute-start.16 = (f32[4,2,128,128]{3,2,1,0:T(8,128)S(1)}, f32[4,2,128,128]{3,2,1,0:T(8,128)S(1)}, u32[]{:S(2)}, u32[]{:S(2)}) collective-permute-start(f32[4,2,128,128]{3,2,1,0:T(8,128)S(1)} %get-tuple-element.59.refs_3_), channel_id=1, source_target_pairs={{1,2},{2,1},{3,6},{6,3},{7,4},{4,7},{9,10},{10,9},{11,14},{14,11},... | collective-permute-start | bytes 1572872 | tf_op jit(solution)/shard_map/ppermute | solution.py:36
  78.6 16.2 %collective-permute-start.17 = (f32[4,2,128,128]{3,2,1,0:T(8,128)S(1)}, f32[4,2,128,128]{3,2,1,0:T(8,128)S(1)}, u32[]{:S(2)}, u32[]{:S(2)}) collective-permute-start(f32[4,2,128,128]{3,2,1,0:T(8,128)S(1)} %get-tuple-element.62.refs_1_), channel_id=1, source_target_pairs={{0,1},{1,0},{2,3},{3,2},{4,5},{5,4},{6,7},{7,6},{8,9},{9,8},{10,11... | collective-permute-start | bytes 1572872 | tf_op jit(solution)/shard_map/ppermute | solution.py:31
  78.6 16.1 %collective-permute-start.18 = (f32[4,2,128,128]{3,2,1,0:T(8,128)S(1)}, f32[4,2,128,128]{3,2,1,0:T(8,128)S(1)}, u32[]{:S(2)}, u32[]{:S(2)}) collective-permute-start(f32[4,2,128,128]{3,2,1,0:T(8,128)S(1)} %get-tuple-element.63.refs_3_), channel_id=1, source_target_pairs={{1,2},{2,1},{3,6},{6,3},{7,4},{4,7},{9,10},{10,9},{11,14},{14,11},... | collective-permute-start | bytes 1572872 | tf_op jit(solution)/shard_map/ppermute | solution.py:36
  81.5 11.1 %collective-permute-start.20 = (f32[2,128,128]{2,1,0:T(8,128)S(1)}, f32[2,128,128]{2,1,0:T(8,128)S(1)}, u32[]{:S(2)}, u32[]{:S(2)}) collective-permute-start(f32[2,128,128]{2,1,0:T(8,128)S(1)} %get-tuple-element.103.refs_6_), channel_id=1, source_target_pairs={{0,8},{8,16},{16,24},{24,0},{1,9},{9,17},{17,25},{25,1},{2,10},{10... | collective-permute-start | bytes 393224 | tf_op jit(solution)/shard_map/ppermute | solution.py:48
  84.0 10.0 %collective-permute-start.21 = (f32[2,128,128]{2,1,0:T(8,128)S(1)}, f32[2,128,128]{2,1,0:T(8,128)S(1)}, u32[]{:S(2)}, u32[]{:S(2)}) collective-permute-start(f32[2,128,128]{2,1,0:T(8,128)S(1)} %get-tuple-element.103.refs_6_), channel_id=1, source_target_pairs={{0,16},{8,24},{16,0},{24,8},{1,17},{9,25},{17,1},{25,9},{2,18},{10... | collective-permute-start | bytes 393224 | tf_op jit(solution)/shard_map/ppermute | solution.py:48
  103.0 11.8 %collective-permute-start.24 = (f32[4,2,128,128]{3,2,1,0:T(8,128)S(1)}, f32[4,2,128,128]{3,2,1,0:T(8,128)S(1)}, u32[]{:S(2)}, u32[]{:S(2)}) collective-permute-start(f32[4,2,128,128]{3,2,1,0:T(8,128)S(1)} %get-tuple-element.66.refs_3_), channel_id=1, source_target_pairs={{1,2},{2,1},{3,6},{6,3},{7,4},{4,7},{9,10},{10,9},{11,14},{14,11},... | collective-permute-start | bytes 1572872 | tf_op jit(solution)/shard_map/ppermute | solution.py:36
  107.9 16.1 %collective-permute-start.25 = (f32[4,2,128,128]{3,2,1,0:T(8,128)S(1)}, f32[4,2,128,128]{3,2,1,0:T(8,128)S(1)}, u32[]{:S(2)}, u32[]{:S(2)}) collective-permute-start(f32[4,2,128,128]{3,2,1,0:T(8,128)S(1)} %get-tuple-element.69.refs_1_), channel_id=1, source_target_pairs={{0,1},{1,0},{2,3},{3,2},{4,5},{5,4},{6,7},{7,6},{8,9},{9,8},{10,11... | collective-permute-start | bytes 1572872 | tf_op jit(solution)/shard_map/ppermute | solution.py:31
  108.0 16.0 %collective-permute-start.26 = (f32[4,2,128,128]{3,2,1,0:T(8,128)S(1)}, f32[4,2,128,128]{3,2,1,0:T(8,128)S(1)}, u32[]{:S(2)}, u32[]{:S(2)}) collective-permute-start(f32[4,2,128,128]{3,2,1,0:T(8,128)S(1)} %get-tuple-element.70.refs_3_), channel_id=1, source_target_pairs={{1,2},{2,1},{3,6},{6,3},{7,4},{4,7},{9,10},{10,9},{11,14},{14,11},... | collective-permute-start | bytes 1572872 | tf_op jit(solution)/shard_map/ppermute | solution.py:36
  110.5 11.1 %collective-permute-start.27 = (f32[2,128,128]{2,1,0:T(8,128)S(1)}, f32[2,128,128]{2,1,0:T(8,128)S(1)}, u32[]{:S(2)}, u32[]{:S(2)}) collective-permute-start(f32[2,128,128]{2,1,0:T(8,128)S(1)} %get-tuple-element.102.refs_6_), channel_id=1, source_target_pairs={{0,8},{8,16},{16,24},{24,0},{1,9},{9,17},{17,25},{25,1},{2,10},{10... | collective-permute-start | bytes 393224 | tf_op jit(solution)/shard_map/ppermute | solution.py:48
  110.6 11.0 %collective-permute-start.28 = (f32[2,128,128]{2,1,0:T(8,128)S(1)}, f32[2,128,128]{2,1,0:T(8,128)S(1)}, u32[]{:S(2)}, u32[]{:S(2)}) collective-permute-start(f32[2,128,128]{2,1,0:T(8,128)S(1)} %get-tuple-element.102.refs_6_), channel_id=1, source_target_pairs={{0,16},{8,24},{16,0},{24,8},{1,17},{9,25},{17,1},{25,9},{2,18},{10... | collective-permute-start | bytes 393224 | tf_op jit(solution)/shard_map/ppermute | solution.py:48
  132.3 11.7 %collective-permute-start.31 = (f32[4,2,128,128]{3,2,1,0:T(8,128)S(1)}, f32[4,2,128,128]{3,2,1,0:T(8,128)S(1)}, u32[]{:S(2)}, u32[]{:S(2)}) collective-permute-start(f32[4,2,128,128]{3,2,1,0:T(8,128)S(1)} %get-tuple-element.73.refs_3_), channel_id=1, source_target_pairs={{1,2},{2,1},{3,6},{6,3},{7,4},{4,7},{9,10},{10,9},{11,14},{14,11},... | collective-permute-start | bytes 1572872 | tf_op jit(solution)/shard_map/ppermute | solution.py:36
  137.1 15.1 %collective-permute-start.32 = (f32[4,2,128,128]{3,2,1,0:T(8,128)S(1)}, f32[4,2,128,128]{3,2,1,0:T(8,128)S(1)}, u32[]{:S(2)}, u32[]{:S(2)}) collective-permute-start(f32[4,2,128,128]{3,2,1,0:T(8,128)S(1)} %get-tuple-element.76.refs_1_), channel_id=1, source_target_pairs={{0,1},{1,0},{2,3},{3,2},{4,5},{5,4},{6,7},{7,6},{8,9},{9,8},{10,11... | collective-permute-start | bytes 1572872 | tf_op jit(solution)/shard_map/ppermute | solution.py:31
  137.2 15.0 %collective-permute-start.33 = (f32[4,2,128,128]{3,2,1,0:T(8,128)S(1)}, f32[4,2,128,128]{3,2,1,0:T(8,128)S(1)}, u32[]{:S(2)}, u32[]{:S(2)}) collective-permute-start(f32[4,2,128,128]{3,2,1,0:T(8,128)S(1)} %get-tuple-element.77.refs_3_), channel_id=1, source_target_pairs={{1,2},{2,1},{3,6},{6,3},{7,4},{4,7},{9,10},{10,9},{11,14},{14,11},... | collective-permute-start | bytes 1572872 | tf_op jit(solution)/shard_map/ppermute | solution.py:36
  160.5 11.8 %collective-permute-start.38 = (f32[4,2,128,128]{3,2,1,0:T(8,128)S(1)}, f32[4,2,128,128]{3,2,1,0:T(8,128)S(1)}, u32[]{:S(2)}, u32[]{:S(2)}) collective-permute-start(f32[4,2,128,128]{3,2,1,0:T(8,128)S(1)} %get-tuple-element.80.refs_3_), channel_id=1, source_target_pairs={{1,2},{2,1},{3,6},{6,3},{7,4},{4,7},{9,10},{10,9},{11,14},{14,11},... | collective-permute-start | bytes 1572872 | tf_op jit(solution)/shard_map/ppermute | solution.py:36
  165.4 15.1 %collective-permute-start.39 = (f32[4,2,128,128]{3,2,1,0:T(8,128)S(1)}, f32[4,2,128,128]{3,2,1,0:T(8,128)S(1)}, u32[]{:S(2)}, u32[]{:S(2)}) collective-permute-start(f32[4,2,128,128]{3,2,1,0:T(8,128)S(1)} %get-tuple-element.83.refs_1_), channel_id=1, source_target_pairs={{0,1},{1,0},{2,3},{3,2},{4,5},{5,4},{6,7},{7,6},{8,9},{9,8},{10,11... | collective-permute-start | bytes 1572872 | tf_op jit(solution)/shard_map/ppermute | solution.py:31
  165.5 15.0 %collective-permute-start.40 = (f32[4,2,128,128]{3,2,1,0:T(8,128)S(1)}, f32[4,2,128,128]{3,2,1,0:T(8,128)S(1)}, u32[]{:S(2)}, u32[]{:S(2)}) collective-permute-start(f32[4,2,128,128]{3,2,1,0:T(8,128)S(1)} %get-tuple-element.84.refs_3_), channel_id=1, source_target_pairs={{1,2},{2,1},{3,6},{6,3},{7,4},{4,7},{9,10},{10,9},{11,14},{14,11},... | collective-permute-start | bytes 1572872 | tf_op jit(solution)/shard_map/ppermute | solution.py:36
  188.8 11.8 %collective-permute-start.45 = (f32[4,2,128,128]{3,2,1,0:T(8,128)S(1)}, f32[4,2,128,128]{3,2,1,0:T(8,128)S(1)}, u32[]{:S(2)}, u32[]{:S(2)}) collective-permute-start(f32[4,2,128,128]{3,2,1,0:T(8,128)S(1)} %get-tuple-element.87.refs_3_), channel_id=1, source_target_pairs={{1,2},{2,1},{3,6},{6,3},{7,4},{4,7},{9,10},{10,9},{11,14},{14,11},... | collective-permute-start | bytes 1572872 | tf_op jit(solution)/shard_map/ppermute | solution.py:36
  193.7 15.0 %collective-permute-start.46 = (f32[4,2,128,128]{3,2,1,0:T(8,128)S(1)}, f32[4,2,128,128]{3,2,1,0:T(8,128)S(1)}, u32[]{:S(2)}, u32[]{:S(2)}) collective-permute-start(f32[4,2,128,128]{3,2,1,0:T(8,128)S(1)} %get-tuple-element.90.refs_0_), channel_id=1, source_target_pairs={{0,1},{1,0},{2,3},{3,2},{4,5},{5,4},{6,7},{7,6},{8,9},{9,8},{10,11... | collective-permute-start | bytes 1572872 | tf_op jit(solution)/shard_map/ppermute | solution.py:31
  193.8 14.9 %collective-permute-start.47 = (f32[4,2,128,128]{3,2,1,0:T(8,128)S(1)}, f32[4,2,128,128]{3,2,1,0:T(8,128)S(1)}, u32[]{:S(2)}, u32[]{:S(2)}) collective-permute-start(f32[4,2,128,128]{3,2,1,0:T(8,128)S(1)} %get-tuple-element.91.refs_2_), channel_id=1, source_target_pairs={{1,2},{2,1},{3,6},{6,3},{7,4},{4,7},{9,10},{10,9},{11,14},{14,11},... | collective-permute-start | bytes 1572872 | tf_op jit(solution)/shard_map/ppermute | solution.py:36
  (30 other events, 247.9 us)
where the time goes:
time: 237 us; the launch traced here: 236 us
  starting transfers between devices  91.2 us (38%)
  Pallas kernels  85.7 us (36%)
  waiting for transfers between devices  54.2 us (23%)
  local copies, waits for them, and re-layouts  2.7 us (1%)
    pallas_call x23, Pallas kernels, call(): pl.pallas_call(kernel, out_shape=[jax.ShapeDtypeStruct(s, F32) for s in o...  85.7 us
    ppermute x14, starting transfers between devices, swap_cols(): lax.ppermute(value, 'gy', both([(2 * i + 1, 2 * j) for i, j in zip(order,...  50.2 us
    ppermute x24, starting transfers between devices, column(): lax.ppermute(value, 'gx', [(i, (i + k) % size) for i in range(size)])  25.4 us
    ppermute x24, waiting for transfers between devices, column(): lax.ppermute(value, 'gx', [(i, (i + k) % size) for i in range(size)])  25 us
    ppermute x14, waiting for transfers between devices, swap_cols(): lax.ppermute(value, 'gy', both([(2 * i + 1, 2 * j) for i, j in zip(order,...  18.3 us
    ppermute x5, starting transfers between devices, place_tiles(): lax.ppermute(value, 'gy', [(2 * i + m, 2 * j + m) for i, j in enumerate(o...  14.4 us
    ppermute x5, waiting for transfers between devices, place_tiles(): lax.ppermute(value, 'gy', [(2 * i + m, 2 * j + m) for i, j in enumerate(o...  10.8 us
  transfers between devices with their start and end apart: 57, of which 23 were waited for; matrix products, arithmetic and copies ran while one was open for 0% of the time, Pallas kernels for 20%

commit v1 on v0

--- a/solution.py
+++ b/solution.py
@@ -99,16 +99,14 @@
     return tuple(jnp.concatenate([a[:, i : i + n] for i in range(0, a.shape[1], n)], 0) for a in x)
 
 
-def there_and_back(x, tab, between):
-    n = x.shape[2]
+def there_and_back(x, tab, wave):
+    count = x.shape[1] // x.shape[2]
 
     def one(inverse, _):
-        y = stack(left(side(right((x[0], x[1]), tab, inverse)), tab, inverse))
+        y = left(side(right((x[0], x[1]), tab, inverse)), tab, inverse)
+        z = cmul(tiled(wave, count), y)
+        y = stack(tuple(jnp.where(inverse == 0, z[p], y[p]) for p in range(2)))
         x[0], x[1] = y
-
-        @pl.when(inverse == 0)
-        def _():
-            lax.fori_loop(0, x.shape[1] // n, lambda s, _: between(s), None)
 
     lax.fori_loop(0, 2, one, None)
 
@@ -193,26 +191,24 @@
                     out[k, p] = scatter(grads, masks, tiles, k, slot, p)
 
 
-def scatter_all(grads, outs, info, offsets, sizes, period):
-    tiles, n = sizes[0], grads.shape[2]
-
-    def block(k):
-        total = [[0.0, 0.0], [0.0, 0.0]]
+def scatter_all(fields, info, offsets, sizes, period):
+    tiles, n = sizes[0], fields[0][0].shape[2]
+
+    def write(k, _):
+        row_sum, near = [[0.0, 0.0] for _ in fields], [[0.0, 0.0] for _ in fields]
         for j, half in ((k, 0), (jnp.where(k == tiles - 1, 0, k + 1), 1)):
             for m in range(BATCH):
                 masks = masks_of(info, offsets, sizes, j, period * BATCH + m, n)
-                grad = load(grads, j * BATCH + m)
-                for p in range(2):
-                    g = jnp.where(masks[half], grad[p], 0.0)
-                    for slot in range(2):
-                        total[slot][p] = total[slot][p] + pick(masks[2], slot, g)
-        return total
-
-    def write(k, _):
-        total = block(k)
-        for slot in range(2):
+                for i, (grads, _, _) in enumerate(fields):
+                    grad = load(grads, j * BATCH + m)
+                    for p in range(2):
+                        g = jnp.where(masks[half], grad[p], 0.0)
+                        row_sum[i][p] = row_sum[i][p] + g
+                        near[i][p] = near[i][p] + jnp.where(masks[2], g, 0.0)
+        for i, (_, slot0, slot1) in enumerate(fields):
             for p in range(2):
-                outs[slot][k, p] = total[slot][p]
+                slot0[k, p] = near[i][p]
+                slot1[k, p] = row_sum[i][p] - near[i][p]
 
     lax.fori_loop(0, tiles, write, None)
 
@@ -263,7 +259,7 @@
             save(inner, j * BATCH + m, cmul((probe[j, m, 0], probe[j, m, 1]), patch))
 
     lax.fori_loop(0, sizes[0], enter, None)
-    there_and_back(inner, tab, lambda s: save(inner, s, cmul(load(inner, s), (wave[0], wave[1]))))
+    there_and_back(inner, tab, wave)
 
 
 def kernel_g(period, sizes, first, tiles, info, offsets, counts, *refs):
@@ -311,11 +307,10 @@
         @pl.when(turn == 0)
         def _():
             lax.fori_loop(0, tiles, exit_plane, None)
-            scatter_all(kept, (he, ho), info, offsets, sizes, period)
 
     lax.fori_loop(0, 2, there_and_back_again, None)
     lax.fori_loop(0, tiles, entrance_plane, None)
-    scatter_all(x, (ge, go), info, offsets, sizes, period)
+    scatter_all(((x, ge, go), (kept, he, ho)), info, offsets, sizes, period)
 
 
 def kernel_b(period, sizes, tiles, info, offsets, counts, obj_in, *refs):

time: 237 us -> 236 us (level)
  transfers between devices with their start and end apart: 57 -> 57, of which waited for: 23 -> 23; matrix products, arithmetic and copies ran while one was open for 0% -> 0% of each run, Pallas kernels for 20% -> 19%
where the time goes in v1:
time: 236 us; the launch traced here: 235 us
  starting transfers between devices  91.3 us (39%)
  Pallas kernels  83.9 us (36%)
  waiting for transfers between devices  54.7 us (23%)
  local copies, waits for them, and re-layouts  2.7 us (1%)
    pallas_call x23, Pallas kernels, call(): pl.pallas_call(kernel, out_shape=[jax.ShapeDtypeStruct(s, F32) for s in o...  83.9 us
    ppermute x14, starting transfers between devices, swap_cols(): lax.ppermute(value, 'gy', both([(2 * i + 1, 2 * j) for i, j in zip(order,...  50.4 us
    ppermute x24, waiting for transfers between devices, column(): lax.ppermute(value, 'gx', [(i, (i + k) % size) for i in range(size)])  25.5 us
    ppermute x24, starting transfers between devices, column(): lax.ppermute(value, 'gx', [(i, (i + k) % size) for i in range(size)])  25.3 us
    ppermute x14, waiting for transfers between devices, swap_cols(): lax.ppermute(value, 'gy', both([(2 * i + 1, 2 * j) for i, j in zip(order,...  18.4 us
    ppermute x5, starting transfers between devices, place_tiles(): lax.ppermute(value, 'gy', [(2 * i + m, 2 * j + m) for i, j in enumerate(o...  14.4 us
    ppermute x5, waiting for transfers between devices, place_tiles(): lax.ppermute(value, 'gy', [(2 * i + m, 2 * j + m) for i, j in enumerate(o...  10.8 us
  transfers between devices with their start and end apart: 57, of which 23 were waited for; matrix products, arithmetic and copies ran while one was open for 0% of the time, Pallas kernels for 19%

profile of v1, /device:TPU:12, one launch (start us, length us, event | category | flops | bytes accessed | tf_op | source)
XLA Modules:
  0.0 235.0 jit_solution(7732353655392410577)
XLA Ops:
  1.9 3.4 %collective-permute-start.6 = (f32[4,128,128]{2,1,0:T(8,128)S(1)}, f32[4,128,128]{2,1,0:T(8,128)S(1)}, u32[]{:S(2)}, u32[]{:S(2)}) collective-permute-start(f32[4,128,128]{2,1,0:T(8,128)S(1)} %pad_maximum_fusion), channel_id=1, source_target_pairs={{0,0},{1,1},{2,2},{3,3},{4,6},{5,7},{6,4},{7,5},{8,8},{9,9},{10,10... | collective-permute-start | bytes 786440 | tf_op jit(solution)/shard_map/ppermute | solution.py:41
  8.8 6.0 %collective-permute-done = f32[264,128]{1,0:T(8,128)S(1)} collective-permute-done((f32[264,128]{1,0:T(8,128)S(1)}, f32[264,128]{1,0:T(8,128)S(1)}, u32[]{:S(2)}, u32[]{:S(2)}) %collective-permute-start) | collective-permute-done | bytes 135200 | tf_op jit(solution)/shard_map/ppermute | solution.py:41
  19.8 3.6 %collective-permute-start.8 = (f32[2,128,128]{2,1,0:T(8,128)S(1)}, f32[2,128,128]{2,1,0:T(8,128)S(1)}, u32[]{:S(2)}, u32[]{:S(2)}) collective-permute-start(f32[2,128,128]{2,1,0:T(8,128)S(1)} %get-tuple-element.105.refs_0_), channel_id=1, source_target_pairs={{0,16},{8,24},{16,0},{24,8},{1,17},{9,25},{17,1},{25,9},{2,18},{10... | collective-permute-start | bytes 393224 | tf_op jit(solution)/shard_map/ppermute | solution.py:48
  26.0 8.5 %collective-permute-done.2 = f32[264,128]{1,0:T(8,128)S(1)} collective-permute-done((f32[264,128]{1,0:T(8,128)S(1)}, f32[264,128]{1,0:T(8,128)S(1)}, u32[]{:S(2)}, u32[]{:S(2)}) %collective-permute-start.2) | collective-permute-done | bytes 135200 | tf_op jit(solution)/shard_map/ppermute | solution.py:48
  44.0 3.1 %collective-permute-start.11 = (f32[4,2,128,128]{3,2,1,0:T(8,128)S(1)}, f32[4,2,128,128]{3,2,1,0:T(8,128)S(1)}, u32[]{:S(2)}, u32[]{:S(2)}) collective-permute-start(f32[4,2,128,128]{3,2,1,0:T(8,128)S(1)} %get-tuple-element.56.refs_2_), channel_id=1, source_target_pairs={{1,2},{2,1},{3,6},{6,3},{7,4},{4,7},{9,10},{10,9},{11,14},{14,11},... | collective-permute-start | bytes 1572872 | tf_op jit(solution)/shard_map/ppermute | solution.py:36
  47.5 2.8 %collective-permute-start.13 = (f32[2,128,128]{2,1,0:T(8,128)S(1)}, f32[2,128,128]{2,1,0:T(8,128)S(1)}, u32[]{:S(2)}, u32[]{:S(2)}) collective-permute-start(f32[2,128,128]{2,1,0:T(8,128)S(1)} %get-tuple-element.104.refs_5_), channel_id=1, source_target_pairs={{0,16},{8,24},{16,0},{24,8},{1,17},{9,25},{17,1},{25,9},{2,18},{10... | collective-permute-start | bytes 393224 | tf_op jit(solution)/shard_map/ppermute | solution.py:48
  53.1 4.6 %shard_map.102 = (f32[4,2,2,128,128]{4,3,2,1,0:T(8,128)S(1)}, f32[2,1024,128]{2,1,0:T(8,128)S(1)}) custom-call(s32[2]{0:T(128)S(1)} %pad_add_fusion.info, s32[4,24]{1,0:T(4,128)S(1)} %bitcast.23, f32[4,2,128,128]{3,2,1,0:T(8,128)S(1)} %get-tuple-element.52.refs_0_, f32[4,2,128,128]{3,2,1,0:T(8,128)S(1)} %collective-permute-done.4.refs_1_, ...), custom_call_target="tpu_custom_call" | custom-call | tf_op jit(solution)/shard_map/pallas_call | solution.py:394
  57.7 9.9 %collective-permute-done.11.refs_3_ = f32[4,2,128,128]{3,2,1,0:T(8,128)S(1)} collective-permute-done((f32[4,2,128,128]{3,2,1,0:T(8,128)S(1)}, f32[4,2,128,128]{3,2,1,0:T(8,128)S(1)}, u32[]{:S(2)}, u32[]{:S(2)}) %collective-permute-start.11) | collective-permute-done | bytes 524320 | tf_op jit(solution)/shard_map/ppermute | solution.py:36
  67.6 7.8 %shard_map.104 = (f32[4,2,2,128,128]{4,3,2,1,0:T(8,128)S(1)}, f32[4,2,128,128]{3,2,1,0:T(8,128)S(1)}, f32[4,2,128,128]{3,2,1,0:T(8,128)S(1)}, f32[4,2,128,128]{3,2,1,0:T(8,128)S(1)}, f32[4,2,128,128]{3,2,1,0:T(8,128)S(1)}) custom-call(s32[2]{0:T(128)S(1)} %pad_add_fusion.info, s32[4,24]{1,0:T(4,128)S(1)} %bitcast.24, s32[4]{0:T(128)S(1)} %slice_reduce_fusion.counts, ...), custom_call_target="tpu_custom_call" | custom-call | tf_op jit(solution)/shard_map/pallas_call | solution.py:394
  87.2 4.7 %shard_map.106 = (f32[4,2,2,128,128]{4,3,2,1,0:T(8,128)S(1)}, f32[2,1024,128]{2,1,0:T(8,128)S(1)}) custom-call(s32[2]{0:T(128)S(1)} %pad_add_fusion.info, s32[4,24]{1,0:T(4,128)S(1)} %bitcast.26, f32[4,2,2,128,128]{4,3,2,1,0:T(8,128)S(1)} %get-tuple-element.54.refs_0_, f32[4,2,128,128]{3,2,1,0:T(8,128)S(1)} %get-tuple-element.58.refs_1_, ...), custom_call_target="tpu_custom_call" | custom-call | tf_op jit(solution)/shard_map/pallas_call | solution.py:394
  94.6 7.9 %shard_map.107 = (f32[4,2,2,128,128]{4,3,2,1,0:T(8,128)S(1)}, f32[4,2,128,128]{3,2,1,0:T(8,128)S(1)}, f32[4,2,128,128]{3,2,1,0:T(8,128)S(1)}, f32[4,2,128,128]{3,2,1,0:T(8,128)S(1)}, f32[4,2,128,128]{3,2,1,0:T(8,128)S(1)}) custom-call(s32[2]{0:T(128)S(1)} %pad_add_fusion.info, s32[4,24]{1,0:T(4,128)S(1)} %bitcast.27, s32[4]{0:T(128)S(1)} %slice_reduce_fusion.counts, ...), custom_call_target="tpu_custom_call" | custom-call | tf_op jit(solution)/shard_map/pallas_call | solution.py:394
  102.6 4.9 %collective-permute-start.24 = (f32[4,2,128,128]{3,2,1,0:T(8,128)S(1)}, f32[4,2,128,128]{3,2,1,0:T(8,128)S(1)}, u32[]{:S(2)}, u32[]{:S(2)}) collective-permute-start(f32[4,2,128,128]{3,2,1,0:T(8,128)S(1)} %get-tuple-element.66.refs_3_), channel_id=1, source_target_pairs={{1,2},{2,1},{3,6},{6,3},{7,4},{4,7},{9,10},{10,9},{11,14},{14,11},... | collective-permute-start | bytes 1572872 | tf_op jit(solution)/shard_map/ppermute | solution.py:36
  110.1 3.2 %collective-permute-start.28 = (f32[2,128,128]{2,1,0:T(8,128)S(1)}, f32[2,128,128]{2,1,0:T(8,128)S(1)}, u32[]{:S(2)}, u32[]{:S(2)}) collective-permute-start(f32[2,128,128]{2,1,0:T(8,128)S(1)} %get-tuple-element.102.refs_6_), channel_id=1, source_target_pairs={{0,16},{8,24},{16,0},{24,8},{1,17},{9,25},{17,1},{25,9},{2,18},{10... | collective-permute-start | bytes 393224 | tf_op jit(solution)/shard_map/ppermute | solution.py:48
  116.4 4.6 %shard_map.109 = (f32[4,2,2,128,128]{4,3,2,1,0:T(8,128)S(1)}, f32[2,1024,128]{2,1,0:T(8,128)S(1)}) custom-call(s32[2]{0:T(128)S(1)} %pad_add_fusion.info, s32[4,24]{1,0:T(4,128)S(1)} %bitcast.29, f32[4,2,2,128,128]{4,3,2,1,0:T(8,128)S(1)} %get-tuple-element.60.refs_0_, f32[4,2,128,128]{3,2,1,0:T(8,128)S(1)} %get-tuple-element.65.refs_1_, ...), custom_call_target="tpu_custom_call" | custom-call | tf_op jit(solution)/shard_map/pallas_call | solution.py:394
  123.6 8.0 %shard_map.110 = (f32[4,2,2,128,128]{4,3,2,1,0:T(8,128)S(1)}, f32[4,2,128,128]{3,2,1,0:T(8,128)S(1)}, f32[4,2,128,128]{3,2,1,0:T(8,128)S(1)}, f32[4,2,128,128]{3,2,1,0:T(8,128)S(1)}, f32[4,2,128,128]{3,2,1,0:T(8,128)S(1)}) custom-call(s32[2]{0:T(128)S(1)} %pad_add_fusion.info, s32[4,24]{1,0:T(4,128)S(1)} %bitcast.30, s32[4]{0:T(128)S(1)} %slice_reduce_fusion.counts, ...), custom_call_target="tpu_custom_call" | custom-call | tf_op jit(solution)/shard_map/pallas_call | solution.py:394
  131.6 4.8 %collective-permute-start.31 = (f32[4,2,128,128]{3,2,1,0:T(8,128)S(1)}, f32[4,2,128,128]{3,2,1,0:T(8,128)S(1)}, u32[]{:S(2)}, u32[]{:S(2)}) collective-permute-start(f32[4,2,128,128]{3,2,1,0:T(8,128)S(1)} %get-tuple-element.73.refs_3_), channel_id=1, source_target_pairs={{1,2},{2,1},{3,6},{6,3},{7,4},{4,7},{9,10},{10,9},{11,14},{14,11},... | collective-permute-start | bytes 1572872 | tf_op jit(solution)/shard_map/ppermute | solution.py:36
  136.5 2.9 %collective-permute-start.33 = (f32[4,2,128,128]{3,2,1,0:T(8,128)S(1)}, f32[4,2,128,128]{3,2,1,0:T(8,128)S(1)}, u32[]{:S(2)}, u32[]{:S(2)}) collective-permute-start(f32[4,2,128,128]{3,2,1,0:T(8,128)S(1)} %get-tuple-element.77.refs_3_), channel_id=1, source_target_pairs={{1,2},{2,1},{3,6},{6,3},{7,4},{4,7},{9,10},{10,9},{11,14},{14,11},... | collective-permute-start | bytes 1572872 | tf_op jit(solution)/shard_map/ppermute | solution.py:36
  144.5 4.6 %shard_map.112 = (f32[4,2,2,128,128]{4,3,2,1,0:T(8,128)S(1)}, f32[2,1024,128]{2,1,0:T(8,128)S(1)}) custom-call(s32[2]{0:T(128)S(1)} %pad_add_fusion.info, s32[4,24]{1,0:T(4,128)S(1)} %bitcast.32, f32[4,2,2,128,128]{4,3,2,1,0:T(8,128)S(1)} %get-tuple-element.67.refs_0_, f32[4,2,128,128]{3,2,1,0:T(8,128)S(1)} %get-tuple-element.72.refs_1_, ...), custom_call_target="tpu_custom_call" | custom-call | tf_op jit(solution)/shard_map/pallas_call | solution.py:394
  151.5 7.9 %shard_map.113 = (f32[4,2,2,128,128]{4,3,2,1,0:T(8,128)S(1)}, f32[4,2,128,128]{3,2,1,0:T(8,128)S(1)}, f32[4,2,128,128]{3,2,1,0:T(8,128)S(1)}, f32[4,2,128,128]{3,2,1,0:T(8,128)S(1)}, f32[4,2,128,128]{3,2,1,0:T(8,128)S(1)}) custom-call(s32[2]{0:T(128)S(1)} %pad_add_fusion.info, s32[4,24]{1,0:T(4,128)S(1)} %bitcast.33, s32[4]{0:T(128)S(1)} %slice_reduce_fusion.counts, ...), custom_call_target="tpu_custom_call" | custom-call | tf_op jit(solution)/shard_map/pallas_call | solution.py:394
  159.5 4.9 %collective-permute-start.38 = (f32[4,2,128,128]{3,2,1,0:T(8,128)S(1)}, f32[4,2,128,128]{3,2,1,0:T(8,128)S(1)}, u32[]{:S(2)}, u32[]{:S(2)}) collective-permute-start(f32[4,2,128,128]{3,2,1,0:T(8,128)S(1)} %get-tuple-element.80.refs_3_), channel_id=1, source_target_pairs={{1,2},{2,1},{3,6},{6,3},{7,4},{4,7},{9,10},{10,9},{11,14},{14,11},... | collective-permute-start | bytes 1572872 | tf_op jit(solution)/shard_map/ppermute | solution.py:36
  164.5 3.0 %collective-permute-start.40 = (f32[4,2,128,128]{3,2,1,0:T(8,128)S(1)}, f32[4,2,128,128]{3,2,1,0:T(8,128)S(1)}, u32[]{:S(2)}, u32[]{:S(2)}) collective-permute-start(f32[4,2,128,128]{3,2,1,0:T(8,128)S(1)} %get-tuple-element.84.refs_3_), channel_id=1, source_target_pairs={{1,2},{2,1},{3,6},{6,3},{7,4},{4,7},{9,10},{10,9},{11,14},{14,11},... | collective-permute-start | bytes 1572872 | tf_op jit(solution)/shard_map/ppermute | solution.py:36
  172.4 4.6 %shard_map.115 = (f32[4,2,2,128,128]{4,3,2,1,0:T(8,128)S(1)}, f32[2,1024,128]{2,1,0:T(8,128)S(1)}) custom-call(s32[2]{0:T(128)S(1)} %pad_add_fusion.info, s32[4,24]{1,0:T(4,128)S(1)} %bitcast.35, f32[4,2,2,128,128]{4,3,2,1,0:T(8,128)S(1)} %get-tuple-element.74.refs_0_, f32[4,2,128,128]{3,2,1,0:T(8,128)S(1)} %get-tuple-element.79.refs_1_, ...), custom_call_target="tpu_custom_call" | custom-call | tf_op jit(solution)/shard_map/pallas_call | solution.py:394
  179.5 8.0 %shard_map.116 = (f32[4,2,2,128,128]{4,3,2,1,0:T(8,128)S(1)}, f32[4,2,128,128]{3,2,1,0:T(8,128)S(1)}, f32[4,2,128,128]{3,2,1,0:T(8,128)S(1)}, f32[4,2,128,128]{3,2,1,0:T(8,128)S(1)}, f32[4,2,128,128]{3,2,1,0:T(8,128)S(1)}) custom-call(s32[2]{0:T(128)S(1)} %pad_add_fusion.info, s32[4,24]{1,0:T(4,128)S(1)} %bitcast.36, s32[4]{0:T(128)S(1)} %slice_reduce_fusion.counts, ...), custom_call_target="tpu_custom_call" | custom-call | tf_op jit(solution)/shard_map/pallas_call | solution.py:394
  187.6 4.9 %collective-permute-start.45 = (f32[4,2,128,128]{3,2,1,0:T(8,128)S(1)}, f32[4,2,128,128]{3,2,1,0:T(8,128)S(1)}, u32[]{:S(2)}, u32[]{:S(2)}) collective-permute-start(f32[4,2,128,128]{3,2,1,0:T(8,128)S(1)} %get-tuple-element.87.refs_3_), channel_id=1, source_target_pairs={{1,2},{2,1},{3,6},{6,3},{7,4},{4,7},{9,10},{10,9},{11,14},{14,11},... | collective-permute-start | bytes 1572872 | tf_op jit(solution)/shard_map/ppermute | solution.py:36
  192.6 3.0 %collective-permute-start.47 = (f32[4,2,128,128]{3,2,1,0:T(8,128)S(1)}, f32[4,2,128,128]{3,2,1,0:T(8,128)S(1)}, u32[]{:S(2)}, u32[]{:S(2)}) collective-permute-start(f32[4,2,128,128]{3,2,1,0:T(8,128)S(1)} %get-tuple-element.91.refs_2_), channel_id=1, source_target_pairs={{1,2},{2,1},{3,6},{6,3},{7,4},{4,7},{9,10},{10,9},{11,14},{14,11},... | collective-permute-start | bytes 1572872 | tf_op jit(solution)/shard_map/ppermute | solution.py:36
  200.5 4.7 %shard_map.118 = (f32[4,2,2,128,128]{4,3,2,1,0:T(8,128)S(1)}, f32[2,1024,128]{2,1,0:T(8,128)S(1)}) custom-call(s32[2]{0:T(128)S(1)} %pad_add_fusion.info, s32[4,24]{1,0:T(4,128)S(1)} %bitcast.38, f32[4,2,2,128,128]{4,3,2,1,0:T(8,128)S(1)} %get-tuple-element.81.refs_0_, f32[4,2,128,128]{3,2,1,0:T(8,128)S(1)} %get-tuple-element.86.refs_1_, ...), custom_call_target="tpu_custom_call" | custom-call | tf_op jit(solution)/shard_map/pallas_call | solution.py:394
  207.5 3.5 %shard_map.119 = (f32[4,2,2,128,128]{4,3,2,1,0:T(8,128)S(1)}, f32[2,1024,128]{2,1,0:T(8,128)S(1)}, f32[2,128,128]{2,1,0:T(8,128)S(1)}, f32[2,128,128]{2,1,0:T(8,128)S(1)}) custom-call(s32[2]{0:T(128)S(1)} %pad_add_fusion.info, s32[4,24]{1,0:T(4,128)S(1)} %bitcast.39, s32[4]{0:T(128)S(1)} %slice_reduce_fusion.counts, ...), custom_call_target="tpu_custom_call" | custom-call | tf_op jit(solution)/shard_map/pallas_call | solution.py:394
  211.0 3.2 %shard_map.120 = (f32[2,128,128]{2,1,0:T(8,128)S(1)}, f32[2,128,128]{2,1,0:T(8,128)S(1)}) custom-call(s32[2]{0:T(128)S(1)} %pad_add_fusion.info, s32[4,24]{1,0:T(4,128)S(1)} %bitcast.40, s32[4]{0:T(128)S(1)} %slice_reduce_fusion.counts, f32[2,1024,128]{2,1,0:T(8,128)S(1)} %get-tuple-element.93.back, f32[4,2,2,128,128]{4,3,2,1,0:T(8,128)S(1)} %shard_map.117.refs_5_.probe, ...), custom_call_target="tpu_custom_call" | custom-call | tf_op jit(solution)/shard_map/pallas_call | solution.py:394
  214.3 4.9 %collective-permute-start.52 = (f32[2,128,128]{2,1,0:T(8,128)S(1)}, f32[2,128,128]{2,1,0:T(8,128)S(1)}, u32[]{:S(2)}, u32[]{:S(2)}) collective-permute-start(f32[2,128,128]{2,1,0:T(8,128)S(1)} %get-tuple-element.95.fo), channel_id=1, source_target_pairs={{1,2},{2,1},{3,6},{6,3},{7,4},{4,7},{9,10},{10,9},{11,14},{14,11},... | collective-permute-start | bytes 393224 | tf_op jit(solution)/shard_map/ppermute | solution.py:36
  219.3 3.0 %collective-permute-start.55 = (f32[2,128,128]{2,1,0:T(8,128)S(1)}, f32[2,128,128]{2,1,0:T(8,128)S(1)}, u32[]{:S(2)}, u32[]{:S(2)}) collective-permute-start(f32[2,128,128]{2,1,0:T(8,128)S(1)} %get-tuple-element.98.fo), channel_id=1, source_target_pairs={{1,2},{2,1},{3,6},{6,3},{7,4},{4,7},{9,10},{10,9},{11,14},{14,11},... | collective-permute-start | bytes 393224 | tf_op jit(solution)/shard_map/ppermute | solution.py:36
  223.0 3.1 %collective-permute-start.53 = (f32[2,128,128]{2,1,0:T(8,128)S(1)}, f32[2,128,128]{2,1,0:T(8,128)S(1)}, u32[]{:S(2)}, u32[]{:S(2)}) collective-permute-start(f32[2,128,128]{2,1,0:T(8,128)S(1)} %shard_map.121), channel_id=1, source_target_pairs={{0,0},{1,1},{2,2},{3,3},{4,6},{5,7},{6,4},{7,5},{8,8},{9,9},{10,10... | collective-permute-start | bytes 393224 | tf_op jit(solution)/shard_map/ppermute | solution.py:41
  230.2 4.0 %collective-permute-done.56 = f32[2,128,128]{2,1,0:T(8,128)S(1)} collective-permute-done((f32[2,128,128]{2,1,0:T(8,128)S(1)}, f32[2,128,128]{2,1,0:T(8,128)S(1)}, u32[]{:S(2)}, u32[]{:S(2)}) %collective-permute-start.56) | collective-permute-done | bytes 131104 | tf_op jit(solution)/shard_map/ppermute | solution.py:41
  (141 shorter events, 75.3 us)
Async XLA Ops:
  1.9 17.5 %collective-permute-start.6 = (f32[4,128,128]{2,1,0:T(8,128)S(1)}, f32[4,128,128]{2,1,0:T(8,128)S(1)}, u32[]{:S(2)}, u32[]{:S(2)}) collective-permute-start(f32[4,128,128]{2,1,0:T(8,128)S(1)} %pad_maximum_fusion), channel_id=1, source_target_pairs={{0,0},{1,1},{2,2},{3,3},{4,6},{5,7},{6,4},{7,5},{8,8},{9,9},{10,10... | collective-permute-start | bytes 786440 | tf_op jit(solution)/shard_map/ppermute | solution.py:41
  14.8 11.2 %collective-permute-start.1 = (f32[264,128]{1,0:T(8,128)S(1)}, f32[264,128]{1,0:T(8,128)S(1)}, u32[]{:S(2)}, u32[]{:S(2)}) collective-permute-start(f32[264,128]{1,0:T(8,128)S(1)} %collective-permute-done), channel_id=1, source_target_pairs={{0,8},{8,16},{16,24},{24,0},{1,9},{9,17},{17,25},{25,1},{2,10},{10... | collective-permute-start | bytes 405512 | tf_op jit(solution)/shard_map/ppermute | solution.py:48
  16.4 18.1 %collective-permute-start.2 = (f32[264,128]{1,0:T(8,128)S(1)}, f32[264,128]{1,0:T(8,128)S(1)}, u32[]{:S(2)}, u32[]{:S(2)}) collective-permute-start(f32[264,128]{1,0:T(8,128)S(1)} %collective-permute-done), channel_id=1, source_target_pairs={{0,16},{8,24},{16,0},{24,8},{1,17},{9,25},{17,1},{25,9},{2,18},{10... | collective-permute-start | bytes 405512 | tf_op jit(solution)/shard_map/ppermute | solution.py:48
  17.6 18.3 %collective-permute-start.3 = (f32[264,128]{1,0:T(8,128)S(1)}, f32[264,128]{1,0:T(8,128)S(1)}, u32[]{:S(2)}, u32[]{:S(2)}) collective-permute-start(f32[264,128]{1,0:T(8,128)S(1)} %collective-permute-done), channel_id=1, source_target_pairs={{0,24},{8,0},{16,8},{24,16},{1,25},{9,1},{17,9},{25,17},{2,26},{10... | collective-permute-start | bytes 405512 | tf_op jit(solution)/shard_map/ppermute | solution.py:48
  19.4 18.0 %collective-permute-start.7 = (f32[2,128,128]{2,1,0:T(8,128)S(1)}, f32[2,128,128]{2,1,0:T(8,128)S(1)}, u32[]{:S(2)}, u32[]{:S(2)}) collective-permute-start(f32[2,128,128]{2,1,0:T(8,128)S(1)} %get-tuple-element.105.refs_0_), channel_id=1, source_target_pairs={{0,8},{8,16},{16,24},{24,0},{1,9},{9,17},{17,25},{25,1},{2,10},{10... | collective-permute-start | bytes 393224 | tf_op jit(solution)/shard_map/ppermute | solution.py:48
  19.8 20.5 %collective-permute-start.8 = (f32[2,128,128]{2,1,0:T(8,128)S(1)}, f32[2,128,128]{2,1,0:T(8,128)S(1)}, u32[]{:S(2)}, u32[]{:S(2)}) collective-permute-start(f32[2,128,128]{2,1,0:T(8,128)S(1)} %get-tuple-element.105.refs_0_), channel_id=1, source_target_pairs={{0,16},{8,24},{16,0},{24,8},{1,17},{9,25},{17,1},{25,9},{2,18},{10... | collective-permute-start | bytes 393224 | tf_op jit(solution)/shard_map/ppermute | solution.py:48
  26.0 17.1 %collective-permute-start.9 = (f32[2,128,128]{2,1,0:T(8,128)S(1)}, f32[2,128,128]{2,1,0:T(8,128)S(1)}, u32[]{:S(2)}, u32[]{:S(2)}) collective-permute-start(f32[2,128,128]{2,1,0:T(8,128)S(1)} %get-tuple-element.105.refs_0_), channel_id=1, source_target_pairs={{0,24},{8,0},{16,8},{24,16},{1,25},{9,1},{17,9},{25,17},{2,26},{10... | collective-permute-start | bytes 393224 | tf_op jit(solution)/shard_map/ppermute | solution.py:48
  36.7 10.8 %collective-permute-start.4 = (f32[4,2,128,128]{3,2,1,0:T(8,128)S(1)}, f32[4,2,128,128]{3,2,1,0:T(8,128)S(1)}, u32[]{:S(2)}, u32[]{:S(2)}) collective-permute-start(f32[4,2,128,128]{3,2,1,0:T(8,128)S(1)} %get-tuple-element.52.refs_0_), channel_id=1, source_target_pairs={{0,1},{1,0},{2,3},{3,2},{4,5},{5,4},{6,7},{7,6},{8,9},{9,8},{10,11... | collective-permute-start | bytes 1572872 | tf_op jit(solution)/shard_map/ppermute | solution.py:31
  37.5 12.9 %collective-permute-start.5 = (f32[4,2,128,128]{3,2,1,0:T(8,128)S(1)}, f32[4,2,128,128]{3,2,1,0:T(8,128)S(1)}, u32[]{:S(2)}, u32[]{:S(2)}) collective-permute-start(f32[4,2,128,128]{3,2,1,0:T(8,128)S(1)} %get-tuple-element.53.refs_2_), channel_id=1, source_target_pairs={{1,2},{2,1},{3,6},{6,3},{7,4},{4,7},{9,10},{10,9},{11,14},{14,11},... | collective-permute-start | bytes 1572872 | tf_op jit(solution)/shard_map/ppermute | solution.py:36
  40.3 40.9 %collective-permute-start.19 = (f32[10,128,128]{2,1,0:T(8,128)S(1)}, f32[10,128,128]{2,1,0:T(8,128)S(1)}, u32[]{:S(2)}, u32[]{:S(2)}) collective-permute-start(f32[10,128,128]{2,1,0:T(8,128)S(1)} %slice_bitcast_fusion), channel_id=1, source_target_pairs={{0,0},{1,1},{2,2},{3,3},{4,6},{5,7},{6,4},{7,5},{8,8},{9,9},{10,10... | collective-permute-start | bytes 1966088 | tf_op jit(solution)/shard_map/ppermute | solution.py:41
  43.8 13.9 %collective-permute-start.10 = (f32[4,2,128,128]{3,2,1,0:T(8,128)S(1)}, f32[4,2,128,128]{3,2,1,0:T(8,128)S(1)}, u32[]{:S(2)}, u32[]{:S(2)}) collective-permute-start(f32[4,2,128,128]{3,2,1,0:T(8,128)S(1)} %get-tuple-element.55.refs_0_), channel_id=1, source_target_pairs={{0,1},{1,0},{2,3},{3,2},{4,5},{5,4},{6,7},{7,6},{8,9},{9,8},{10,11... | collective-permute-start | bytes 1572872 | tf_op jit(solution)/shard_map/ppermute | solution.py:31
  44.0 23.6 %collective-permute-start.11 = (f32[4,2,128,128]{3,2,1,0:T(8,128)S(1)}, f32[4,2,128,128]{3,2,1,0:T(8,128)S(1)}, u32[]{:S(2)}, u32[]{:S(2)}) collective-permute-start(f32[4,2,128,128]{3,2,1,0:T(8,128)S(1)} %get-tuple-element.56.refs_2_), channel_id=1, source_target_pairs={{1,2},{2,1},{3,6},{6,3},{7,4},{4,7},{9,10},{10,9},{11,14},{14,11},... | collective-permute-start | bytes 1572872 | tf_op jit(solution)/shard_map/ppermute | solution.py:36
  47.5 10.2 %collective-permute-start.13 = (f32[2,128,128]{2,1,0:T(8,128)S(1)}, f32[2,128,128]{2,1,0:T(8,128)S(1)}, u32[]{:S(2)}, u32[]{:S(2)}) collective-permute-start(f32[2,128,128]{2,1,0:T(8,128)S(1)} %get-tuple-element.104.refs_5_), channel_id=1, source_target_pairs={{0,16},{8,24},{16,0},{24,8},{1,17},{9,25},{17,1},{25,9},{2,18},{10... | collective-permute-start | bytes 393224 | tf_op jit(solution)/shard_map/ppermute | solution.py:48
  75.5 10.5 %collective-permute-start.16 = (f32[4,2,128,128]{3,2,1,0:T(8,128)S(1)}, f32[4,2,128,128]{3,2,1,0:T(8,128)S(1)}, u32[]{:S(2)}, u32[]{:S(2)}) collective-permute-start(f32[4,2,128,128]{3,2,1,0:T(8,128)S(1)} %get-tuple-element.59.refs_3_), channel_id=1, source_target_pairs={{1,2},{2,1},{3,6},{6,3},{7,4},{4,7},{9,10},{10,9},{11,14},{14,11},... | collective-permute-start | bytes 1572872 | tf_op jit(solution)/shard_map/ppermute | solution.py:36
  78.3 16.2 %collective-permute-start.17 = (f32[4,2,128,128]{3,2,1,0:T(8,128)S(1)}, f32[4,2,128,128]{3,2,1,0:T(8,128)S(1)}, u32[]{:S(2)}, u32[]{:S(2)}) collective-permute-start(f32[4,2,128,128]{3,2,1,0:T(8,128)S(1)} %get-tuple-element.62.refs_1_), channel_id=1, source_target_pairs={{0,1},{1,0},{2,3},{3,2},{4,5},{5,4},{6,7},{7,6},{8,9},{9,8},{10,11... | collective-permute-start | bytes 1572872 | tf_op jit(solution)/shard_map/ppermute | solution.py:31
  78.4 16.1 %collective-permute-start.18 = (f32[4,2,128,128]{3,2,1,0:T(8,128)S(1)}, f32[4,2,128,128]{3,2,1,0:T(8,128)S(1)}, u32[]{:S(2)}, u32[]{:S(2)}) collective-permute-start(f32[4,2,128,128]{3,2,1,0:T(8,128)S(1)} %get-tuple-element.63.refs_3_), channel_id=1, source_target_pairs={{1,2},{2,1},{3,6},{6,3},{7,4},{4,7},{9,10},{10,9},{11,14},{14,11},... | collective-permute-start | bytes 1572872 | tf_op jit(solution)/shard_map/ppermute | solution.py:36
  81.3 11.1 %collective-permute-start.20 = (f32[2,128,128]{2,1,0:T(8,128)S(1)}, f32[2,128,128]{2,1,0:T(8,128)S(1)}, u32[]{:S(2)}, u32[]{:S(2)}) collective-permute-start(f32[2,128,128]{2,1,0:T(8,128)S(1)} %get-tuple-element.103.refs_6_), channel_id=1, source_target_pairs={{0,8},{8,16},{16,24},{24,0},{1,9},{9,17},{17,25},{25,1},{2,10},{10... | collective-permute-start | bytes 393224 | tf_op jit(solution)/shard_map/ppermute | solution.py:48
  83.8 10.0 %collective-permute-start.21 = (f32[2,128,128]{2,1,0:T(8,128)S(1)}, f32[2,128,128]{2,1,0:T(8,128)S(1)}, u32[]{:S(2)}, u32[]{:S(2)}) collective-permute-start(f32[2,128,128]{2,1,0:T(8,128)S(1)} %get-tuple-element.103.refs_6_), channel_id=1, source_target_pairs={{0,16},{8,24},{16,0},{24,8},{1,17},{9,25},{17,1},{25,9},{2,18},{10... | collective-permute-start | bytes 393224 | tf_op jit(solution)/shard_map/ppermute | solution.py:48
  102.6 11.8 %collective-permute-start.24 = (f32[4,2,128,128]{3,2,1,0:T(8,128)S(1)}, f32[4,2,128,128]{3,2,1,0:T(8,128)S(1)}, u32[]{:S(2)}, u32[]{:S(2)}) collective-permute-start(f32[4,2,128,128]{3,2,1,0:T(8,128)S(1)} %get-tuple-element.66.refs_3_), channel_id=1, source_target_pairs={{1,2},{2,1},{3,6},{6,3},{7,4},{4,7},{9,10},{10,9},{11,14},{14,11},... | collective-permute-start | bytes 1572872 | tf_op jit(solution)/shard_map/ppermute | solution.py:36
  107.5 16.1 %collective-permute-start.25 = (f32[4,2,128,128]{3,2,1,0:T(8,128)S(1)}, f32[4,2,128,128]{3,2,1,0:T(8,128)S(1)}, u32[]{:S(2)}, u32[]{:S(2)}) collective-permute-start(f32[4,2,128,128]{3,2,1,0:T(8,128)S(1)} %get-tuple-element.69.refs_1_), channel_id=1, source_target_pairs={{0,1},{1,0},{2,3},{3,2},{4,5},{5,4},{6,7},{7,6},{8,9},{9,8},{10,11... | collective-permute-start | bytes 1572872 | tf_op jit(solution)/shard_map/ppermute | solution.py:31
  107.6 16.0 %collective-permute-start.26 = (f32[4,2,128,128]{3,2,1,0:T(8,128)S(1)}, f32[4,2,128,128]{3,2,1,0:T(8,128)S(1)}, u32[]{:S(2)}, u32[]{:S(2)}) collective-permute-start(f32[4,2,128,128]{3,2,1,0:T(8,128)S(1)} %get-tuple-element.70.refs_3_), channel_id=1, source_target_pairs={{1,2},{2,1},{3,6},{6,3},{7,4},{4,7},{9,10},{10,9},{11,14},{14,11},... | collective-permute-start | bytes 1572872 | tf_op jit(solution)/shard_map/ppermute | solution.py:36
  110.1 11.0 %collective-permute-start.27 = (f32[2,128,128]{2,1,0:T(8,128)S(1)}, f32[2,128,128]{2,1,0:T(8,128)S(1)}, u32[]{:S(2)}, u32[]{:S(2)}) collective-permute-start(f32[2,128,128]{2,1,0:T(8,128)S(1)} %get-tuple-element.102.refs_6_), channel_id=1, source_target_pairs={{0,8},{8,16},{16,24},{24,0},{1,9},{9,17},{17,25},{25,1},{2,10},{10... | collective-permute-start | bytes 393224 | tf_op jit(solution)/shard_map/ppermute | solution.py:48
  110.1 10.9 %collective-permute-start.28 = (f32[2,128,128]{2,1,0:T(8,128)S(1)}, f32[2,128,128]{2,1,0:T(8,128)S(1)}, u32[]{:S(2)}, u32[]{:S(2)}) collective-permute-start(f32[2,128,128]{2,1,0:T(8,128)S(1)} %get-tuple-element.102.refs_6_), channel_id=1, source_target_pairs={{0,16},{8,24},{16,0},{24,8},{1,17},{9,25},{17,1},{25,9},{2,18},{10... | collective-permute-start | bytes 393224 | tf_op jit(solution)/shard_map/ppermute | solution.py:48
  131.6 11.7 %collective-permute-start.31 = (f32[4,2,128,128]{3,2,1,0:T(8,128)S(1)}, f32[4,2,128,128]{3,2,1,0:T(8,128)S(1)}, u32[]{:S(2)}, u32[]{:S(2)}) collective-permute-start(f32[4,2,128,128]{3,2,1,0:T(8,128)S(1)} %get-tuple-element.73.refs_3_), channel_id=1, source_target_pairs={{1,2},{2,1},{3,6},{6,3},{7,4},{4,7},{9,10},{10,9},{11,14},{14,11},... | collective-permute-start | bytes 1572872 | tf_op jit(solution)/shard_map/ppermute | solution.py:36
  136.5 15.0 %collective-permute-start.32 = (f32[4,2,128,128]{3,2,1,0:T(8,128)S(1)}, f32[4,2,128,128]{3,2,1,0:T(8,128)S(1)}, u32[]{:S(2)}, u32[]{:S(2)}) collective-permute-start(f32[4,2,128,128]{3,2,1,0:T(8,128)S(1)} %get-tuple-element.76.refs_1_), channel_id=1, source_target_pairs={{0,1},{1,0},{2,3},{3,2},{4,5},{5,4},{6,7},{7,6},{8,9},{9,8},{10,11... | collective-permute-start | bytes 1572872 | tf_op jit(solution)/shard_map/ppermute | solution.py:31
  136.5 14.9 %collective-permute-start.33 = (f32[4,2,128,128]{3,2,1,0:T(8,128)S(1)}, f32[4,2,128,128]{3,2,1,0:T(8,128)S(1)}, u32[]{:S(2)}, u32[]{:S(2)}) collective-permute-start(f32[4,2,128,128]{3,2,1,0:T(8,128)S(1)} %get-tuple-element.77.refs_3_), channel_id=1, source_target_pairs={{1,2},{2,1},{3,6},{6,3},{7,4},{4,7},{9,10},{10,9},{11,14},{14,11},... | collective-permute-start | bytes 1572872 | tf_op jit(solution)/shard_map/ppermute | solution.py:36
  159.5 11.8 %collective-permute-start.38 = (f32[4,2,128,128]{3,2,1,0:T(8,128)S(1)}, f32[4,2,128,128]{3,2,1,0:T(8,128)S(1)}, u32[]{:S(2)}, u32[]{:S(2)}) collective-permute-start(f32[4,2,128,128]{3,2,1,0:T(8,128)S(1)} %get-tuple-element.80.refs_3_), channel_id=1, source_target_pairs={{1,2},{2,1},{3,6},{6,3},{7,4},{4,7},{9,10},{10,9},{11,14},{14,11},... | collective-permute-start | bytes 1572872 | tf_op jit(solution)/shard_map/ppermute | solution.py:36
  164.4 15.1 %collective-permute-start.39 = (f32[4,2,128,128]{3,2,1,0:T(8,128)S(1)}, f32[4,2,128,128]{3,2,1,0:T(8,128)S(1)}, u32[]{:S(2)}, u32[]{:S(2)}) collective-permute-start(f32[4,2,128,128]{3,2,1,0:T(8,128)S(1)} %get-tuple-element.83.refs_1_), channel_id=1, source_target_pairs={{0,1},{1,0},{2,3},{3,2},{4,5},{5,4},{6,7},{7,6},{8,9},{9,8},{10,11... | collective-permute-start | bytes 1572872 | tf_op jit(solution)/shard_map/ppermute | solution.py:31
  164.5 15.0 %collective-permute-start.40 = (f32[4,2,128,128]{3,2,1,0:T(8,128)S(1)}, f32[4,2,128,128]{3,2,1,0:T(8,128)S(1)}, u32[]{:S(2)}, u32[]{:S(2)}) collective-permute-start(f32[4,2,128,128]{3,2,1,0:T(8,128)S(1)} %get-tuple-element.84.refs_3_), channel_id=1, source_target_pairs={{1,2},{2,1},{3,6},{6,3},{7,4},{4,7},{9,10},{10,9},{11,14},{14,11},... | collective-permute-start | bytes 1572872 | tf_op jit(solution)/shard_map/ppermute | solution.py:36
  187.6 11.8 %collective-permute-start.45 = (f32[4,2,128,128]{3,2,1,0:T(8,128)S(1)}, f32[4,2,128,128]{3,2,1,0:T(8,128)S(1)}, u32[]{:S(2)}, u32[]{:S(2)}) collective-permute-start(f32[4,2,128,128]{3,2,1,0:T(8,128)S(1)} %get-tuple-element.87.refs_3_), channel_id=1, source_target_pairs={{1,2},{2,1},{3,6},{6,3},{7,4},{4,7},{9,10},{10,9},{11,14},{14,11},... | collective-permute-start | bytes 1572872 | tf_op jit(solution)/shard_map/ppermute | solution.py:36
  192.5 15.0 %collective-permute-start.46 = (f32[4,2,128,128]{3,2,1,0:T(8,128)S(1)}, f32[4,2,128,128]{3,2,1,0:T(8,128)S(1)}, u32[]{:S(2)}, u32[]{:S(2)}) collective-permute-start(f32[4,2,128,128]{3,2,1,0:T(8,128)S(1)} %get-tuple-element.90.refs_0_), channel_id=1, source_target_pairs={{0,1},{1,0},{2,3},{3,2},{4,5},{5,4},{6,7},{7,6},{8,9},{9,8},{10,11... | collective-permute-start | bytes 1572872 | tf_op jit(solution)/shard_map/ppermute | solution.py:31
  192.6 14.9 %collective-permute-start.47 = (f32[4,2,128,128]{3,2,1,0:T(8,128)S(1)}, f32[4,2,128,128]{3,2,1,0:T(8,128)S(1)}, u32[]{:S(2)}, u32[]{:S(2)}) collective-permute-start(f32[4,2,128,128]{3,2,1,0:T(8,128)S(1)} %get-tuple-element.91.refs_2_), channel_id=1, source_target_pairs={{1,2},{2,1},{3,6},{6,3},{7,4},{4,7},{9,10},{10,9},{11,14},{14,11},... | collective-permute-start | bytes 1572872 | tf_op jit(solution)/shard_map/ppermute | solution.py:36
  (30 other events, 247.1 us)

commit v2 on v1

--- a/solution.py
+++ b/solution.py
@@ -262,6 +262,12 @@
     there_and_back(inner, tab, wave)
 
 
+def levels_of(measured, period):
+    size = measured[0].shape[0]
+    start = period * BATCH % size
+    return jnp.concatenate([x[start + m] for x in measured for m in range(BATCH)], 1)
+
+
 def kernel_g(period, sizes, first, tiles, info, offsets, counts, *refs):
     obj_in = None if first else refs[0]
     refs = refs[0 if first else 1 :]
@@ -296,7 +302,7 @@
 
     def there_and_back_again(turn, _):
         y = left(side(right((x[0], x[1]), tab, 0)), tab, 0)
-        level = jnp.concatenate([measured[j][m] for j in range(tiles) for m in range(BATCH)], 1)
+        level = levels_of(measured, period)
         e = y[0] * y[0] + y[1] * y[1] - level
         q = conj_mul(tiled(wave, count), y)
         z = tuple(jnp.where(turn == 0, e * y[p], q[p]) for p in range(2))
@@ -323,7 +329,7 @@
     waves = rows_of((inner[0], inner[1]), tiles, n)
     x = stacked([[cmul(waves[j][m], seconds[j][m]) for m in range(BATCH)] for j in range(tiles)])
     x = left(side(right(x, tab, 0)), tab, 0)
-    level = jnp.concatenate([measured[j][m] for j in range(tiles) for m in range(BATCH)], 1)
+    level = levels_of(measured, period)
     e = x[0] * x[0] + x[1] * x[1] - level
     x = right(stack(left((e * x[0], e * x[1]), tab, 1)), tab, 1)
     exits = rows_of(x, tiles, n)
@@ -462,8 +468,9 @@
         ro = swap_cols(ho)
         sums1 = [he, swap_core(he), ho, ro]
         probes.append(roll(b + 1))
-        if b + 2 < NB:
-            measured.append(column(own3[(b + 1) * BATCH : (b + 2) * BATCH]))
+        if b % 2 == 0 and b + 2 < NB:
+            pieces = column(own3[(b + 1) * BATCH : (b + 3) * BATCH])
+            measured += [pieces, pieces]
     b = NB - 1
     out1, back, he, ho = call(
         functools.partial(kernel_b, b, sizes, tiles), [info, offs, count],

time: 236 us -> 240 us (1.017)
  waiting for transfers between devices: 54.7 us -> 66.7 us
  starting transfers between devices: 91.3 us -> 83.8 us
    ppermute x24 -> x18, waiting for transfers between devices: 25.5 us -> 42.5 us  [column(): lax.ppermute(value, 'gx', [(i, (i + k) % size) for i in range(size)])]
    ppermute x24 -> x18, starting transfers between devices: 25.3 us -> 19.6 us  [column(): lax.ppermute(value, 'gx', [(i, (i + k) % size) for i in range(size)])]
    ppermute x14, waiting for transfers between devices: 18.4 us -> 13.1 us  [swap_cols(): lax.ppermute(value, 'gy', both([(2 * i + 1, 2 * j) for i, j in zip(order,...]
  transfers between devices with their start and end apart: 57 -> 51, of which waited for: 23 -> 22; matrix products, arithmetic and copies ran while one was open for 0% -> 0% of each run, Pallas kernels for 19% -> 19%
where the time goes in v2:
time: 240 us
  starting transfers between devices  83.8 us (35%)
  Pallas kernels  83.8 us (35%)
  waiting for transfers between devices  66.7 us (28%)
  local copies, waits for them, and re-layouts  2.71 us (1%)
    pallas_call x23, Pallas kernels, call(): pl.pallas_call(kernel, out_shape=[jax.ShapeDtypeStruct(s, F32) for s in o...  83.8 us
    ppermute x14, starting transfers between devices, swap_cols(): lax.ppermute(value, 'gy', both([(2 * i + 1, 2 * j) for i, j in zip(order,...  49.1 us
    ppermute x18, waiting for transfers between devices, column(): lax.ppermute(value, 'gx', [(i, (i + k) % size) for i in range(size)])  42.5 us
    ppermute x18, starting transfers between devices, column(): lax.ppermute(value, 'gx', [(i, (i + k) % size) for i in range(size)])  19.6 us
    ppermute x5, starting transfers between devices, place_tiles(): lax.ppermute(value, 'gy', [(2 * i + m, 2 * j + m) for i, j in enumerate(o...  14.1 us
    ppermute x14, waiting for transfers between devices, swap_cols(): lax.ppermute(value, 'gy', both([(2 * i + 1, 2 * j) for i, j in zip(order,...  13.1 us
    ppermute x5, waiting for transfers between devices, place_tiles(): lax.ppermute(value, 'gy', [(2 * i + m, 2 * j + m) for i, j in enumerate(o...  11.1 us
  transfers between devices with their start and end apart: 51, of which 22 were waited for; matrix products, arithmetic and copies ran while one was open for 0% of the time, Pallas kernels for 19%

profile of v2, /device:TPU:12, one launch (start us, length us, event | category | flops | bytes accessed | tf_op | source)
XLA Modules:
  0.0 239.5 jit_solution(1067105696775427831)
XLA Ops:
  1.9 3.4 %collective-permute-start.6 = (f32[4,128,128]{2,1,0:T(8,128)S(1)}, f32[4,128,128]{2,1,0:T(8,128)S(1)}, u32[]{:S(2)}, u32[]{:S(2)}) collective-permute-start(f32[4,128,128]{2,1,0:T(8,128)S(1)} %pad_maximum_fusion), channel_id=1, source_target_pairs={{0,0},{1,1},{2,2},{3,3},{4,6},{5,7},{6,4},{7,5},{8,8},{9,9},{10,10... | collective-permute-start | bytes 786440 | tf_op jit(solution)/shard_map/ppermute | solution.py:41
  8.9 5.9 %collective-permute-done = f32[264,128]{1,0:T(8,128)S(1)} collective-permute-done((f32[264,128]{1,0:T(8,128)S(1)}, f32[264,128]{1,0:T(8,128)S(1)}, u32[]{:S(2)}, u32[]{:S(2)}) %collective-permute-start) | collective-permute-done | bytes 135200 | tf_op jit(solution)/shard_map/ppermute | solution.py:41
  19.7 3.5 %collective-permute-start.8 = (f32[2,128,128]{2,1,0:T(8,128)S(1)}, f32[2,128,128]{2,1,0:T(8,128)S(1)}, u32[]{:S(2)}, u32[]{:S(2)}) collective-permute-start(f32[2,128,128]{2,1,0:T(8,128)S(1)} %get-tuple-element.102.refs_0_), channel_id=1, source_target_pairs={{0,16},{8,24},{16,0},{24,8},{1,17},{9,25},{17,1},{25,9},{2,18},{10... | collective-permute-start | bytes 393224 | tf_op jit(solution)/shard_map/ppermute | solution.py:48
  26.0 8.6 %collective-permute-done.2 = f32[264,128]{1,0:T(8,128)S(1)} collective-permute-done((f32[264,128]{1,0:T(8,128)S(1)}, f32[264,128]{1,0:T(8,128)S(1)}, u32[]{:S(2)}, u32[]{:S(2)}) %collective-permute-start.2) | collective-permute-done | bytes 135200 | tf_op jit(solution)/shard_map/ppermute | solution.py:48
  35.5 3.5 %collective-permute-start.5 = (f32[4,2,128,128]{3,2,1,0:T(8,128)S(1)}, f32[4,2,128,128]{3,2,1,0:T(8,128)S(1)}, u32[]{:S(2)}, u32[]{:S(2)}) collective-permute-start(f32[4,2,128,128]{3,2,1,0:T(8,128)S(1)} %get-tuple-element.53.refs_2_), channel_id=1, source_target_pairs={{1,2},{2,1},{3,6},{6,3},{7,4},{4,7},{9,10},{10,9},{11,14},{14,11},... | collective-permute-start | bytes 1572872 | tf_op jit(solution)/shard_map/ppermute | solution.py:36
  40.9 3.5 %collective-permute-start.11 = (f32[4,2,128,128]{3,2,1,0:T(8,128)S(1)}, f32[4,2,128,128]{3,2,1,0:T(8,128)S(1)}, u32[]{:S(2)}, u32[]{:S(2)}) collective-permute-start(f32[4,2,128,128]{3,2,1,0:T(8,128)S(1)} %get-tuple-element.56.refs_2_), channel_id=1, source_target_pairs={{1,2},{2,1},{3,6},{6,3},{7,4},{4,7},{9,10},{10,9},{11,14},{14,11},... | collective-permute-start | bytes 1572872 | tf_op jit(solution)/shard_map/ppermute | solution.py:36
  47.0 3.4 %collective-permute-start.13 = (f32[2,128,128]{2,1,0:T(8,128)S(1)}, f32[2,128,128]{2,1,0:T(8,128)S(1)}, u32[]{:S(2)}, u32[]{:S(2)}) collective-permute-start(f32[2,128,128]{2,1,0:T(8,128)S(1)} %get-tuple-element.101.refs_5_), channel_id=1, source_target_pairs={{0,16},{8,24},{16,0},{24,8},{1,17},{9,25},{17,1},{25,9},{2,18},{10... | collective-permute-start | bytes 393224 | tf_op jit(solution)/shard_map/ppermute | solution.py:48
  52.4 4.6 %shard_map.102 = (f32[4,2,2,128,128]{4,3,2,1,0:T(8,128)S(1)}, f32[2,1024,128]{2,1,0:T(8,128)S(1)}) custom-call(s32[2]{0:T(128)S(1)} %pad_add_fusion.info, s32[4,24]{1,0:T(4,128)S(1)} %bitcast.23, f32[4,2,128,128]{3,2,1,0:T(8,128)S(1)} %get-tuple-element.52.refs_0_, f32[4,2,128,128]{3,2,1,0:T(8,128)S(1)} %collective-permute-done.4.refs_1_, ...), custom_call_target="tpu_custom_call" | custom-call | tf_op jit(solution)/shard_map/pallas_call | solution.py:400
  59.3 7.8 %shard_map.104 = (f32[4,2,2,128,128]{4,3,2,1,0:T(8,128)S(1)}, f32[4,2,128,128]{3,2,1,0:T(8,128)S(1)}, f32[4,2,128,128]{3,2,1,0:T(8,128)S(1)}, f32[4,2,128,128]{3,2,1,0:T(8,128)S(1)}, f32[4,2,128,128]{3,2,1,0:T(8,128)S(1)}) custom-call(s32[2]{0:T(128)S(1)} %pad_add_fusion.info, s32[4,24]{1,0:T(4,128)S(1)} %bitcast.24, s32[4]{0:T(128)S(1)} %slice_reduce_fusion.counts, ...), custom_call_target="tpu_custom_call" | custom-call | tf_op jit(solution)/shard_map/pallas_call | solution.py:400
  69.6 3.3 %collective-permute-start.18 = (f32[4,2,128,128]{3,2,1,0:T(8,128)S(1)}, f32[4,2,128,128]{3,2,1,0:T(8,128)S(1)}, u32[]{:S(2)}, u32[]{:S(2)}) collective-permute-start(f32[4,2,128,128]{3,2,1,0:T(8,128)S(1)} %get-tuple-element.63.refs_3_), channel_id=1, source_target_pairs={{1,2},{2,1},{3,6},{6,3},{7,4},{4,7},{9,10},{10,9},{11,14},{14,11},... | collective-permute-start | bytes 1572872 | tf_op jit(solution)/shard_map/ppermute | solution.py:36
  79.0 4.6 %shard_map.106 = (f32[4,2,2,128,128]{4,3,2,1,0:T(8,128)S(1)}, f32[2,1024,128]{2,1,0:T(8,128)S(1)}) custom-call(s32[2]{0:T(128)S(1)} %pad_add_fusion.info, s32[4,24]{1,0:T(4,128)S(1)} %bitcast.26, f32[4,2,2,128,128]{4,3,2,1,0:T(8,128)S(1)} %get-tuple-element.54.refs_0_, f32[4,2,128,128]{3,2,1,0:T(8,128)S(1)} %get-tuple-element.58.refs_1_, ...), custom_call_target="tpu_custom_call" | custom-call | tf_op jit(solution)/shard_map/pallas_call | solution.py:400
  85.7 7.9 %shard_map.107 = (f32[4,2,2,128,128]{4,3,2,1,0:T(8,128)S(1)}, f32[4,2,128,128]{3,2,1,0:T(8,128)S(1)}, f32[4,2,128,128]{3,2,1,0:T(8,128)S(1)}, f32[4,2,128,128]{3,2,1,0:T(8,128)S(1)}, f32[4,2,128,128]{3,2,1,0:T(8,128)S(1)}) custom-call(s32[2]{0:T(128)S(1)} %pad_add_fusion.info, s32[4,24]{1,0:T(4,128)S(1)} %bitcast.27, s32[4]{0:T(128)S(1)} %slice_reduce_fusion.counts, ...), custom_call_target="tpu_custom_call" | custom-call | tf_op jit(solution)/shard_map/pallas_call | solution.py:400
  93.7 4.8 %collective-permute-start.24 = (f32[4,2,128,128]{3,2,1,0:T(8,128)S(1)}, f32[4,2,128,128]{3,2,1,0:T(8,128)S(1)}, u32[]{:S(2)}, u32[]{:S(2)}) collective-permute-start(f32[4,2,128,128]{3,2,1,0:T(8,128)S(1)} %get-tuple-element.66.refs_3_), channel_id=1, source_target_pairs={{1,2},{2,1},{3,6},{6,3},{7,4},{4,7},{9,10},{10,9},{11,14},{14,11},... | collective-permute-start | bytes 1572872 | tf_op jit(solution)/shard_map/ppermute | solution.py:36
  107.4 4.7 %shard_map.109 = (f32[4,2,2,128,128]{4,3,2,1,0:T(8,128)S(1)}, f32[2,1024,128]{2,1,0:T(8,128)S(1)}) custom-call(s32[2]{0:T(128)S(1)} %pad_add_fusion.info, s32[4,24]{1,0:T(4,128)S(1)} %bitcast.29, f32[4,2,2,128,128]{4,3,2,1,0:T(8,128)S(1)} %get-tuple-element.60.refs_0_, f32[4,2,128,128]{3,2,1,0:T(8,128)S(1)} %get-tuple-element.65.refs_1_, ...), custom_call_target="tpu_custom_call" | custom-call | tf_op jit(solution)/shard_map/pallas_call | solution.py:400
  112.1 7.0 %collective-permute-done.27.refs_7_ = f32[4,128,128]{2,1,0:T(8,128)S(1)} collective-permute-done((f32[4,128,128]{2,1,0:T(8,128)S(1)}, f32[4,128,128]{2,1,0:T(8,128)S(1)}, u32[]{:S(2)}, u32[]{:S(2)}) %collective-permute-start.27) | collective-permute-done | bytes 262176 | tf_op jit(solution)/shard_map/ppermute | solution.py:48
  119.0 3.7 %collective-permute-done.28.refs_8_ = f32[4,128,128]{2,1,0:T(8,128)S(1)} collective-permute-done((f32[4,128,128]{2,1,0:T(8,128)S(1)}, f32[4,128,128]{2,1,0:T(8,128)S(1)}, u32[]{:S(2)}, u32[]{:S(2)}) %collective-permute-start.28) | collective-permute-done | bytes 262176 | tf_op jit(solution)/shard_map/ppermute | solution.py:48
  124.8 7.9 %shard_map.110 = (f32[4,2,2,128,128]{4,3,2,1,0:T(8,128)S(1)}, f32[4,2,128,128]{3,2,1,0:T(8,128)S(1)}, f32[4,2,128,128]{3,2,1,0:T(8,128)S(1)}, f32[4,2,128,128]{3,2,1,0:T(8,128)S(1)}, f32[4,2,128,128]{3,2,1,0:T(8,128)S(1)}) custom-call(s32[2]{0:T(128)S(1)} %pad_add_fusion.info, s32[4,24]{1,0:T(4,128)S(1)} %bitcast.30, s32[4]{0:T(128)S(1)} %slice_reduce_fusion.counts, ...), custom_call_target="tpu_custom_call" | custom-call | tf_op jit(solution)/shard_map/pallas_call | solution.py:400
  132.9 4.8 %collective-permute-start.31 = (f32[4,2,128,128]{3,2,1,0:T(8,128)S(1)}, f32[4,2,128,128]{3,2,1,0:T(8,128)S(1)}, u32[]{:S(2)}, u32[]{:S(2)}) collective-permute-start(f32[4,2,128,128]{3,2,1,0:T(8,128)S(1)} %get-tuple-element.73.refs_3_), channel_id=1, source_target_pairs={{1,2},{2,1},{3,6},{6,3},{7,4},{4,7},{9,10},{10,9},{11,14},{14,11},... | collective-permute-start | bytes 1572872 | tf_op jit(solution)/shard_map/ppermute | solution.py:36
  137.8 3.6 %collective-permute-start.33 = (f32[4,2,128,128]{3,2,1,0:T(8,128)S(1)}, f32[4,2,128,128]{3,2,1,0:T(8,128)S(1)}, u32[]{:S(2)}, u32[]{:S(2)}) collective-permute-start(f32[4,2,128,128]{3,2,1,0:T(8,128)S(1)} %get-tuple-element.77.refs_3_), channel_id=1, source_target_pairs={{1,2},{2,1},{3,6},{6,3},{7,4},{4,7},{9,10},{10,9},{11,14},{14,11},... | collective-permute-start | bytes 1572872 | tf_op jit(solution)/shard_map/ppermute | solution.py:36
  144.5 4.6 %shard_map.112 = (f32[4,2,2,128,128]{4,3,2,1,0:T(8,128)S(1)}, f32[2,1024,128]{2,1,0:T(8,128)S(1)}) custom-call(s32[2]{0:T(128)S(1)} %pad_add_fusion.info, s32[4,24]{1,0:T(4,128)S(1)} %bitcast.32, f32[4,2,2,128,128]{4,3,2,1,0:T(8,128)S(1)} %get-tuple-element.67.refs_0_, f32[4,2,128,128]{3,2,1,0:T(8,128)S(1)} %get-tuple-element.72.refs_1_, ...), custom_call_target="tpu_custom_call" | custom-call | tf_op jit(solution)/shard_map/pallas_call | solution.py:400
  150.2 7.9 %shard_map.113 = (f32[4,2,2,128,128]{4,3,2,1,0:T(8,128)S(1)}, f32[4,2,128,128]{3,2,1,0:T(8,128)S(1)}, f32[4,2,128,128]{3,2,1,0:T(8,128)S(1)}, f32[4,2,128,128]{3,2,1,0:T(8,128)S(1)}, f32[4,2,128,128]{3,2,1,0:T(8,128)S(1)}) custom-call(s32[2]{0:T(128)S(1)} %pad_add_fusion.info, s32[4,24]{1,0:T(4,128)S(1)} %bitcast.33, s32[4]{0:T(128)S(1)} %slice_reduce_fusion.counts, ...), custom_call_target="tpu_custom_call" | custom-call | tf_op jit(solution)/shard_map/pallas_call | solution.py:400
  158.2 3.7 %collective-permute-start.35 = (f32[4,2,128,128]{3,2,1,0:T(8,128)S(1)}, f32[4,2,128,128]{3,2,1,0:T(8,128)S(1)}, u32[]{:S(2)}, u32[]{:S(2)}) collective-permute-start(f32[4,2,128,128]{3,2,1,0:T(8,128)S(1)} %get-tuple-element.80.refs_3_), channel_id=1, source_target_pairs={{1,2},{2,1},{3,6},{6,3},{7,4},{4,7},{9,10},{10,9},{11,14},{14,11},... | collective-permute-start | bytes 1572872 | tf_op jit(solution)/shard_map/ppermute | solution.py:36
  161.9 3.4 %collective-permute-start.37 = (f32[4,2,128,128]{3,2,1,0:T(8,128)S(1)}, f32[4,2,128,128]{3,2,1,0:T(8,128)S(1)}, u32[]{:S(2)}, u32[]{:S(2)}) collective-permute-start(f32[4,2,128,128]{3,2,1,0:T(8,128)S(1)} %get-tuple-element.84.refs_3_), channel_id=1, source_target_pairs={{1,2},{2,1},{3,6},{6,3},{7,4},{4,7},{9,10},{10,9},{11,14},{14,11},... | collective-permute-start | bytes 1572872 | tf_op jit(solution)/shard_map/ppermute | solution.py:36
  169.9 4.6 %shard_map.115 = (f32[4,2,2,128,128]{4,3,2,1,0:T(8,128)S(1)}, f32[2,1024,128]{2,1,0:T(8,128)S(1)}) custom-call(s32[2]{0:T(128)S(1)} %pad_add_fusion.info, s32[4,24]{1,0:T(4,128)S(1)} %bitcast.35, f32[4,2,2,128,128]{4,3,2,1,0:T(8,128)S(1)} %get-tuple-element.74.refs_0_, f32[4,2,128,128]{3,2,1,0:T(8,128)S(1)} %get-tuple-element.79.refs_1_, ...), custom_call_target="tpu_custom_call" | custom-call | tf_op jit(solution)/shard_map/pallas_call | solution.py:400
  174.5 8.7 %collective-permute-done.38.refs_7_.refs_6_ = f32[4,128,128]{2,1,0:T(8,128)S(1)} collective-permute-done((f32[4,128,128]{2,1,0:T(8,128)S(1)}, f32[4,128,128]{2,1,0:T(8,128)S(1)}, u32[]{:S(2)}, u32[]{:S(2)}) %collective-permute-start.38) | collective-permute-done | bytes 262176 | tf_op jit(solution)/shard_map/ppermute | solution.py:48
  187.9 7.9 %shard_map.116 = (f32[4,2,2,128,128]{4,3,2,1,0:T(8,128)S(1)}, f32[4,2,128,128]{3,2,1,0:T(8,128)S(1)}, f32[4,2,128,128]{3,2,1,0:T(8,128)S(1)}, f32[4,2,128,128]{3,2,1,0:T(8,128)S(1)}, f32[4,2,128,128]{3,2,1,0:T(8,128)S(1)}) custom-call(s32[2]{0:T(128)S(1)} %pad_add_fusion.info, s32[4,24]{1,0:T(4,128)S(1)} %bitcast.36, s32[4]{0:T(128)S(1)} %slice_reduce_fusion.counts, ...), custom_call_target="tpu_custom_call" | custom-call | tf_op jit(solution)/shard_map/pallas_call | solution.py:400
  195.9 4.8 %collective-permute-start.42 = (f32[4,2,128,128]{3,2,1,0:T(8,128)S(1)}, f32[4,2,128,128]{3,2,1,0:T(8,128)S(1)}, u32[]{:S(2)}, u32[]{:S(2)}) collective-permute-start(f32[4,2,128,128]{3,2,1,0:T(8,128)S(1)} %get-tuple-element.87.refs_3_), channel_id=1, source_target_pairs={{1,2},{2,1},{3,6},{6,3},{7,4},{4,7},{9,10},{10,9},{11,14},{14,11},... | collective-permute-start | bytes 1572872 | tf_op jit(solution)/shard_map/ppermute | solution.py:36
  207.6 4.6 %shard_map.118 = (f32[4,2,2,128,128]{4,3,2,1,0:T(8,128)S(1)}, f32[2,1024,128]{2,1,0:T(8,128)S(1)}) custom-call(s32[2]{0:T(128)S(1)} %pad_add_fusion.info, s32[4,24]{1,0:T(4,128)S(1)} %bitcast.38, f32[4,2,2,128,128]{4,3,2,1,0:T(8,128)S(1)} %get-tuple-element.81.refs_0_, f32[4,2,128,128]{3,2,1,0:T(8,128)S(1)} %get-tuple-element.86.refs_1_, ...), custom_call_target="tpu_custom_call" | custom-call | tf_op jit(solution)/shard_map/pallas_call | solution.py:400
  213.2 3.5 %shard_map.119 = (f32[4,2,2,128,128]{4,3,2,1,0:T(8,128)S(1)}, f32[2,1024,128]{2,1,0:T(8,128)S(1)}, f32[2,128,128]{2,1,0:T(8,128)S(1)}, f32[2,128,128]{2,1,0:T(8,128)S(1)}) custom-call(s32[2]{0:T(128)S(1)} %pad_add_fusion.info, s32[4,24]{1,0:T(4,128)S(1)} %bitcast.39, s32[4]{0:T(128)S(1)} %slice_reduce_fusion.counts, ...), custom_call_target="tpu_custom_call" | custom-call | tf_op jit(solution)/shard_map/pallas_call | solution.py:400
  220.0 3.6 %collective-permute-start.46 = (f32[2,128,128]{2,1,0:T(8,128)S(1)}, f32[2,128,128]{2,1,0:T(8,128)S(1)}, u32[]{:S(2)}, u32[]{:S(2)}) collective-permute-start(f32[2,128,128]{2,1,0:T(8,128)S(1)} %get-tuple-element.95.fo), channel_id=1, source_target_pairs={{1,2},{2,1},{3,6},{6,3},{7,4},{4,7},{9,10},{10,9},{11,14},{14,11},... | collective-permute-start | bytes 393224 | tf_op jit(solution)/shard_map/ppermute | solution.py:36
  227.0 4.0 %collective-permute-start.47 = (f32[2,128,128]{2,1,0:T(8,128)S(1)}, f32[2,128,128]{2,1,0:T(8,128)S(1)}, u32[]{:S(2)}, u32[]{:S(2)}) collective-permute-start(f32[2,128,128]{2,1,0:T(8,128)S(1)} %shard_map.121), channel_id=1, source_target_pairs={{0,0},{1,1},{2,2},{3,3},{4,6},{5,7},{6,4},{7,5},{8,8},{9,9},{10,10... | collective-permute-start | bytes 393224 | tf_op jit(solution)/shard_map/ppermute | solution.py:41
  234.7 4.0 %collective-permute-done.50 = f32[2,128,128]{2,1,0:T(8,128)S(1)} collective-permute-done((f32[2,128,128]{2,1,0:T(8,128)S(1)}, f32[2,128,128]{2,1,0:T(8,128)S(1)}, u32[]{:S(2)}, u32[]{:S(2)}) %collective-permute-start.50) | collective-permute-done | bytes 131104 | tf_op jit(solution)/shard_map/ppermute | solution.py:41
  (130 shorter events, 75.7 us)
Async XLA Ops:
  1.9 17.5 %collective-permute-start.6 = (f32[4,128,128]{2,1,0:T(8,128)S(1)}, f32[4,128,128]{2,1,0:T(8,128)S(1)}, u32[]{:S(2)}, u32[]{:S(2)}) collective-permute-start(f32[4,128,128]{2,1,0:T(8,128)S(1)} %pad_maximum_fusion), channel_id=1, source_target_pairs={{0,0},{1,1},{2,2},{3,3},{4,6},{5,7},{6,4},{7,5},{8,8},{9,9},{10,10... | collective-permute-start | bytes 786440 | tf_op jit(solution)/shard_map/ppermute | solution.py:41
  14.8 11.2 %collective-permute-start.1 = (f32[264,128]{1,0:T(8,128)S(1)}, f32[264,128]{1,0:T(8,128)S(1)}, u32[]{:S(2)}, u32[]{:S(2)}) collective-permute-start(f32[264,128]{1,0:T(8,128)S(1)} %collective-permute-done), channel_id=1, source_target_pairs={{0,8},{8,16},{16,24},{24,0},{1,9},{9,17},{17,25},{25,1},{2,10},{10... | collective-permute-start | bytes 405512 | tf_op jit(solution)/shard_map/ppermute | solution.py:48
  16.4 18.3 %collective-permute-start.2 = (f32[264,128]{1,0:T(8,128)S(1)}, f32[264,128]{1,0:T(8,128)S(1)}, u32[]{:S(2)}, u32[]{:S(2)}) collective-permute-start(f32[264,128]{1,0:T(8,128)S(1)} %collective-permute-done), channel_id=1, source_target_pairs={{0,16},{8,24},{16,0},{24,8},{1,17},{9,25},{17,1},{25,9},{2,18},{10... | collective-permute-start | bytes 405512 | tf_op jit(solution)/shard_map/ppermute | solution.py:48
  17.6 17.1 %collective-permute-start.3 = (f32[264,128]{1,0:T(8,128)S(1)}, f32[264,128]{1,0:T(8,128)S(1)}, u32[]{:S(2)}, u32[]{:S(2)}) collective-permute-start(f32[264,128]{1,0:T(8,128)S(1)} %collective-permute-done), channel_id=1, source_target_pairs={{0,24},{8,0},{16,8},{24,16},{1,25},{9,1},{17,9},{25,17},{2,26},{10... | collective-permute-start | bytes 405512 | tf_op jit(solution)/shard_map/ppermute | solution.py:48
  19.5 19.6 %collective-permute-start.7 = (f32[2,128,128]{2,1,0:T(8,128)S(1)}, f32[2,128,128]{2,1,0:T(8,128)S(1)}, u32[]{:S(2)}, u32[]{:S(2)}) collective-permute-start(f32[2,128,128]{2,1,0:T(8,128)S(1)} %get-tuple-element.102.refs_0_), channel_id=1, source_target_pairs={{0,8},{8,16},{16,24},{24,0},{1,9},{9,17},{17,25},{25,1},{2,10},{10... | collective-permute-start | bytes 393224 | tf_op jit(solution)/shard_map/ppermute | solution.py:48
  19.7 19.6 %collective-permute-start.8 = (f32[2,128,128]{2,1,0:T(8,128)S(1)}, f32[2,128,128]{2,1,0:T(8,128)S(1)}, u32[]{:S(2)}, u32[]{:S(2)}) collective-permute-start(f32[2,128,128]{2,1,0:T(8,128)S(1)} %get-tuple-element.102.refs_0_), channel_id=1, source_target_pairs={{0,16},{8,24},{16,0},{24,8},{1,17},{9,25},{17,1},{25,9},{2,18},{10... | collective-permute-start | bytes 393224 | tf_op jit(solution)/shard_map/ppermute | solution.py:48
  26.0 14.0 %collective-permute-start.9 = (f32[2,128,128]{2,1,0:T(8,128)S(1)}, f32[2,128,128]{2,1,0:T(8,128)S(1)}, u32[]{:S(2)}, u32[]{:S(2)}) collective-permute-start(f32[2,128,128]{2,1,0:T(8,128)S(1)} %get-tuple-element.102.refs_0_), channel_id=1, source_target_pairs={{0,24},{8,0},{16,8},{24,16},{1,25},{9,1},{17,9},{25,17},{2,26},{10... | collective-permute-start | bytes 393224 | tf_op jit(solution)/shard_map/ppermute | solution.py:48
  35.4 11.6 %collective-permute-start.4 = (f32[4,2,128,128]{3,2,1,0:T(8,128)S(1)}, f32[4,2,128,128]{3,2,1,0:T(8,128)S(1)}, u32[]{:S(2)}, u32[]{:S(2)}) collective-permute-start(f32[4,2,128,128]{3,2,1,0:T(8,128)S(1)} %get-tuple-element.52.refs_0_), channel_id=1, source_target_pairs={{0,1},{1,0},{2,3},{3,2},{4,5},{5,4},{6,7},{7,6},{8,9},{9,8},{10,11... | collective-permute-start | bytes 1572872 | tf_op jit(solution)/shard_map/ppermute | solution.py:31
  35.5 15.0 %collective-permute-start.5 = (f32[4,2,128,128]{3,2,1,0:T(8,128)S(1)}, f32[4,2,128,128]{3,2,1,0:T(8,128)S(1)}, u32[]{:S(2)}, u32[]{:S(2)}) collective-permute-start(f32[4,2,128,128]{3,2,1,0:T(8,128)S(1)} %get-tuple-element.53.refs_2_), channel_id=1, source_target_pairs={{1,2},{2,1},{3,6},{6,3},{7,4},{4,7},{9,10},{10,9},{11,14},{14,11},... | collective-permute-start | bytes 1572872 | tf_op jit(solution)/shard_map/ppermute | solution.py:36
  40.8 18.5 %collective-permute-start.10 = (f32[4,2,128,128]{3,2,1,0:T(8,128)S(1)}, f32[4,2,128,128]{3,2,1,0:T(8,128)S(1)}, u32[]{:S(2)}, u32[]{:S(2)}) collective-permute-start(f32[4,2,128,128]{3,2,1,0:T(8,128)S(1)} %get-tuple-element.55.refs_0_), channel_id=1, source_target_pairs={{0,1},{1,0},{2,3},{3,2},{4,5},{5,4},{6,7},{7,6},{8,9},{9,8},{10,11... | collective-permute-start | bytes 1572872 | tf_op jit(solution)/shard_map/ppermute | solution.py:31
  40.9 18.4 %collective-permute-start.11 = (f32[4,2,128,128]{3,2,1,0:T(8,128)S(1)}, f32[4,2,128,128]{3,2,1,0:T(8,128)S(1)}, u32[]{:S(2)}, u32[]{:S(2)}) collective-permute-start(f32[4,2,128,128]{3,2,1,0:T(8,128)S(1)} %get-tuple-element.56.refs_2_), channel_id=1, source_target_pairs={{1,2},{2,1},{3,6},{6,3},{7,4},{4,7},{9,10},{10,9},{11,14},{14,11},... | collective-permute-start | bytes 1572872 | tf_op jit(solution)/shard_map/ppermute | solution.py:36
  44.7 28.2 %collective-permute-start.19 = (f32[10,128,128]{2,1,0:T(8,128)S(1)}, f32[10,128,128]{2,1,0:T(8,128)S(1)}, u32[]{:S(2)}, u32[]{:S(2)}) collective-permute-start(f32[10,128,128]{2,1,0:T(8,128)S(1)} %slice_bitcast_fusion), channel_id=1, source_target_pairs={{0,0},{1,1},{2,2},{3,3},{4,6},{5,7},{6,4},{7,5},{8,8},{9,9},{10,10... | collective-permute-start | bytes 1966088 | tf_op jit(solution)/shard_map/ppermute | solution.py:41
  47.0 11.5 %collective-permute-start.13 = (f32[2,128,128]{2,1,0:T(8,128)S(1)}, f32[2,128,128]{2,1,0:T(8,128)S(1)}, u32[]{:S(2)}, u32[]{:S(2)}) collective-permute-start(f32[2,128,128]{2,1,0:T(8,128)S(1)} %get-tuple-element.101.refs_5_), channel_id=1, source_target_pairs={{0,16},{8,24},{16,0},{24,8},{1,17},{9,25},{17,1},{25,9},{2,18},{10... | collective-permute-start | bytes 393224 | tf_op jit(solution)/shard_map/ppermute | solution.py:48
  69.5 16.2 %collective-permute-start.17 = (f32[4,2,128,128]{3,2,1,0:T(8,128)S(1)}, f32[4,2,128,128]{3,2,1,0:T(8,128)S(1)}, u32[]{:S(2)}, u32[]{:S(2)}) collective-permute-start(f32[4,2,128,128]{3,2,1,0:T(8,128)S(1)} %get-tuple-element.62.refs_1_), channel_id=1, source_target_pairs={{0,1},{1,0},{2,3},{3,2},{4,5},{5,4},{6,7},{7,6},{8,9},{9,8},{10,11... | collective-permute-start | bytes 1572872 | tf_op jit(solution)/shard_map/ppermute | solution.py:31
  69.6 16.1 %collective-permute-start.18 = (f32[4,2,128,128]{3,2,1,0:T(8,128)S(1)}, f32[4,2,128,128]{3,2,1,0:T(8,128)S(1)}, u32[]{:S(2)}, u32[]{:S(2)}) collective-permute-start(f32[4,2,128,128]{3,2,1,0:T(8,128)S(1)} %get-tuple-element.63.refs_3_), channel_id=1, source_target_pairs={{1,2},{2,1},{3,6},{6,3},{7,4},{4,7},{9,10},{10,9},{11,14},{14,11},... | collective-permute-start | bytes 1572872 | tf_op jit(solution)/shard_map/ppermute | solution.py:36
  93.7 11.7 %collective-permute-start.24 = (f32[4,2,128,128]{3,2,1,0:T(8,128)S(1)}, f32[4,2,128,128]{3,2,1,0:T(8,128)S(1)}, u32[]{:S(2)}, u32[]{:S(2)}) collective-permute-start(f32[4,2,128,128]{3,2,1,0:T(8,128)S(1)} %get-tuple-element.66.refs_3_), channel_id=1, source_target_pairs={{1,2},{2,1},{3,6},{6,3},{7,4},{4,7},{9,10},{10,9},{11,14},{14,11},... | collective-permute-start | bytes 1572872 | tf_op jit(solution)/shard_map/ppermute | solution.py:36
  98.5 26.3 %collective-permute-start.25 = (f32[4,2,128,128]{3,2,1,0:T(8,128)S(1)}, f32[4,2,128,128]{3,2,1,0:T(8,128)S(1)}, u32[]{:S(2)}, u32[]{:S(2)}) collective-permute-start(f32[4,2,128,128]{3,2,1,0:T(8,128)S(1)} %get-tuple-element.69.refs_1_), channel_id=1, source_target_pairs={{0,1},{1,0},{2,3},{3,2},{4,5},{5,4},{6,7},{7,6},{8,9},{9,8},{10,11... | collective-permute-start | bytes 1572872 | tf_op jit(solution)/shard_map/ppermute | solution.py:31
  98.6 26.2 %collective-permute-start.26 = (f32[4,2,128,128]{3,2,1,0:T(8,128)S(1)}, f32[4,2,128,128]{3,2,1,0:T(8,128)S(1)}, u32[]{:S(2)}, u32[]{:S(2)}) collective-permute-start(f32[4,2,128,128]{3,2,1,0:T(8,128)S(1)} %get-tuple-element.70.refs_3_), channel_id=1, source_target_pairs={{1,2},{2,1},{3,6},{6,3},{7,4},{4,7},{9,10},{10,9},{11,14},{14,11},... | collective-permute-start | bytes 1572872 | tf_op jit(solution)/shard_map/ppermute | solution.py:36
  101.2 17.9 %collective-permute-start.27 = (f32[4,128,128]{2,1,0:T(8,128)S(1)}, f32[4,128,128]{2,1,0:T(8,128)S(1)}, u32[]{:S(2)}, u32[]{:S(2)}) collective-permute-start(f32[4,128,128]{2,1,0:T(8,128)S(1)} %get-tuple-element.100.refs_6_), channel_id=1, source_target_pairs={{0,8},{8,16},{16,24},{24,0},{1,9},{9,17},{17,25},{25,1},{2,10},{10... | collective-permute-start | bytes 786440 | tf_op jit(solution)/shard_map/ppermute | solution.py:48
  101.3 21.5 %collective-permute-start.28 = (f32[4,128,128]{2,1,0:T(8,128)S(1)}, f32[4,128,128]{2,1,0:T(8,128)S(1)}, u32[]{:S(2)}, u32[]{:S(2)}) collective-permute-start(f32[4,128,128]{2,1,0:T(8,128)S(1)} %get-tuple-element.100.refs_6_), channel_id=1, source_target_pairs={{0,16},{8,24},{16,0},{24,8},{1,17},{9,25},{17,1},{25,9},{2,18},{10... | collective-permute-start | bytes 786440 | tf_op jit(solution)/shard_map/ppermute | solution.py:48
  105.4 19.5 %collective-permute-start.29 = (f32[4,128,128]{2,1,0:T(8,128)S(1)}, f32[4,128,128]{2,1,0:T(8,128)S(1)}, u32[]{:S(2)}, u32[]{:S(2)}) collective-permute-start(f32[4,128,128]{2,1,0:T(8,128)S(1)} %get-tuple-element.100.refs_6_), channel_id=1, source_target_pairs={{0,24},{8,0},{16,8},{24,16},{1,25},{9,1},{17,9},{25,17},{2,26},{10... | collective-permute-start | bytes 786440 | tf_op jit(solution)/shard_map/ppermute | solution.py:48
  132.9 11.7 %collective-permute-start.31 = (f32[4,2,128,128]{3,2,1,0:T(8,128)S(1)}, f32[4,2,128,128]{3,2,1,0:T(8,128)S(1)}, u32[]{:S(2)}, u32[]{:S(2)}) collective-permute-start(f32[4,2,128,128]{3,2,1,0:T(8,128)S(1)} %get-tuple-element.73.refs_3_), channel_id=1, source_target_pairs={{1,2},{2,1},{3,6},{6,3},{7,4},{4,7},{9,10},{10,9},{11,14},{14,11},... | collective-permute-start | bytes 1572872 | tf_op jit(solution)/shard_map/ppermute | solution.py:36
  137.7 11.5 %collective-permute-start.32 = (f32[4,2,128,128]{3,2,1,0:T(8,128)S(1)}, f32[4,2,128,128]{3,2,1,0:T(8,128)S(1)}, u32[]{:S(2)}, u32[]{:S(2)}) collective-permute-start(f32[4,2,128,128]{3,2,1,0:T(8,128)S(1)} %get-tuple-element.76.refs_1_), channel_id=1, source_target_pairs={{0,1},{1,0},{2,3},{3,2},{4,5},{5,4},{6,7},{7,6},{8,9},{9,8},{10,11... | collective-permute-start | bytes 1572872 | tf_op jit(solution)/shard_map/ppermute | solution.py:31
  137.8 12.4 %collective-permute-start.33 = (f32[4,2,128,128]{3,2,1,0:T(8,128)S(1)}, f32[4,2,128,128]{3,2,1,0:T(8,128)S(1)}, u32[]{:S(2)}, u32[]{:S(2)}) collective-permute-start(f32[4,2,128,128]{3,2,1,0:T(8,128)S(1)} %get-tuple-element.77.refs_3_), channel_id=1, source_target_pairs={{1,2},{2,1},{3,6},{6,3},{7,4},{4,7},{9,10},{10,9},{11,14},{14,11},... | collective-permute-start | bytes 1572872 | tf_op jit(solution)/shard_map/ppermute | solution.py:36
  161.9 26.0 %collective-permute-start.36 = (f32[4,2,128,128]{3,2,1,0:T(8,128)S(1)}, f32[4,2,128,128]{3,2,1,0:T(8,128)S(1)}, u32[]{:S(2)}, u32[]{:S(2)}) collective-permute-start(f32[4,2,128,128]{3,2,1,0:T(8,128)S(1)} %get-tuple-element.83.refs_1_), channel_id=1, source_target_pairs={{0,1},{1,0},{2,3},{3,2},{4,5},{5,4},{6,7},{7,6},{8,9},{9,8},{10,11... | collective-permute-start | bytes 1572872 | tf_op jit(solution)/shard_map/ppermute | solution.py:31
  161.9 26.0 %collective-permute-start.37 = (f32[4,2,128,128]{3,2,1,0:T(8,128)S(1)}, f32[4,2,128,128]{3,2,1,0:T(8,128)S(1)}, u32[]{:S(2)}, u32[]{:S(2)}) collective-permute-start(f32[4,2,128,128]{3,2,1,0:T(8,128)S(1)} %get-tuple-element.84.refs_3_), channel_id=1, source_target_pairs={{1,2},{2,1},{3,6},{6,3},{7,4},{4,7},{9,10},{10,9},{11,14},{14,11},... | collective-permute-start | bytes 1572872 | tf_op jit(solution)/shard_map/ppermute | solution.py:36
  165.3 17.9 %collective-permute-start.38 = (f32[4,128,128]{2,1,0:T(8,128)S(1)}, f32[4,128,128]{2,1,0:T(8,128)S(1)}, u32[]{:S(2)}, u32[]{:S(2)}) collective-permute-start(f32[4,128,128]{2,1,0:T(8,128)S(1)} %get-tuple-element.99.refs_6_.refs_5_), channel_id=1, source_target_pairs={{0,8},{8,16},{16,24},{24,0},{1,9},{9,17},{17,25},{25,1},{2,10},{10... | collective-permute-start | bytes 786440 | tf_op jit(solution)/shard_map/ppermute | solution.py:48
  165.4 20.6 %collective-permute-start.39 = (f32[4,128,128]{2,1,0:T(8,128)S(1)}, f32[4,128,128]{2,1,0:T(8,128)S(1)}, u32[]{:S(2)}, u32[]{:S(2)}) collective-permute-start(f32[4,128,128]{2,1,0:T(8,128)S(1)} %get-tuple-element.99.refs_6_.refs_5_), channel_id=1, source_target_pairs={{0,16},{8,24},{16,0},{24,8},{1,17},{9,25},{17,1},{25,9},{2,18},{10... | collective-permute-start | bytes 786440 | tf_op jit(solution)/shard_map/ppermute | solution.py:48
  168.7 19.2 %collective-permute-start.40 = (f32[4,128,128]{2,1,0:T(8,128)S(1)}, f32[4,128,128]{2,1,0:T(8,128)S(1)}, u32[]{:S(2)}, u32[]{:S(2)}) collective-permute-start(f32[4,128,128]{2,1,0:T(8,128)S(1)} %get-tuple-element.99.refs_6_.refs_5_), channel_id=1, source_target_pairs={{0,24},{8,0},{16,8},{24,16},{1,25},{9,1},{17,9},{25,17},{2,26},{10... | collective-permute-start | bytes 786440 | tf_op jit(solution)/shard_map/ppermute | solution.py:48
  195.9 11.7 %collective-permute-start.42 = (f32[4,2,128,128]{3,2,1,0:T(8,128)S(1)}, f32[4,2,128,128]{3,2,1,0:T(8,128)S(1)}, u32[]{:S(2)}, u32[]{:S(2)}) collective-permute-start(f32[4,2,128,128]{3,2,1,0:T(8,128)S(1)} %get-tuple-element.87.refs_3_), channel_id=1, source_target_pairs={{1,2},{2,1},{3,6},{6,3},{7,4},{4,7},{9,10},{10,9},{11,14},{14,11},... | collective-permute-start | bytes 1572872 | tf_op jit(solution)/shard_map/ppermute | solution.py:36
  200.8 11.5 %collective-permute-start.43 = (f32[4,2,128,128]{3,2,1,0:T(8,128)S(1)}, f32[4,2,128,128]{3,2,1,0:T(8,128)S(1)}, u32[]{:S(2)}, u32[]{:S(2)}) collective-permute-start(f32[4,2,128,128]{3,2,1,0:T(8,128)S(1)} %get-tuple-element.90.refs_0_), channel_id=1, source_target_pairs={{0,1},{1,0},{2,3},{3,2},{4,5},{5,4},{6,7},{7,6},{8,9},{9,8},{10,11... | collective-permute-start | bytes 1572872 | tf_op jit(solution)/shard_map/ppermute | solution.py:31
  200.8 12.4 %collective-permute-start.44 = (f32[4,2,128,128]{3,2,1,0:T(8,128)S(1)}, f32[4,2,128,128]{3,2,1,0:T(8,128)S(1)}, u32[]{:S(2)}, u32[]{:S(2)}) collective-permute-start(f32[4,2,128,128]{3,2,1,0:T(8,128)S(1)} %get-tuple-element.91.refs_2_), channel_id=1, source_target_pairs={{1,2},{2,1},{3,6},{6,3},{7,4},{4,7},{9,10},{10,9},{11,14},{14,11},... | collective-permute-start | bytes 1572872 | tf_op jit(solution)/shard_map/ppermute | solution.py:36
  (24 other events, 190.9 us)
